TPU v7x, 32 devices: a whole 2x2x4 slice. The times are simulated.
32 devices in a mesh: gx: 8 (over y, x, core), gy: 4 (over z).
Axes of the slice: x: 2, y: 2, z: 4, core: 2. Of those that a mesh axis runs over, the one named last changes fastest.
Arguments:
- density: bfloat16 [2048, 128, 128], P(('gx', 'gy')), may hold values from -0.00390625 to 0.00390625
- dest: int32 [2048, 2], P(('gx', 'gy')), may hold values from 0 to 31, all different within a row; in each aligned block of 64 rows (0 to 63, 64 to 127, ...) at most 8 rows name the same one
- code: int32 [2048, 2], P(('gx', 'gy')), may hold values from 0 to 143
- basis: bfloat16 [65536, 1536], P(('gx', 'gy')), may hold values from -6 to 6
- descriptors: float32 [10, 65536], P(None, ('gx', 'gy')), may hold values from -6 to 6
- weights: float32 [65536], P(('gx', 'gy')), may hold values from 0.0055242717 to 0.198873782
- w_in: float32 [11, 128], replicated, may hold values from -1.75 to 1.75
- w_hid1: float32 [128, 128], replicated, may hold values from -0.5 to 0.5
- w_hid2: float32 [128, 128], replicated, may hold values from -0.5 to 0.5
- w_out: float32 [128], replicated, may hold values from -0.5 to 0.5
Outputs:
- fock: float32 [2048, 128, 128], P(('gx', 'gy'))
- energy: float32 [], replicated
Inputs may be any that keep to these rules, and one draw needn't show every extreme that they name: `dest`: the two copies of a pair block go to different domains; among the pair blocks of one device at most 8 copies go to one domain.
All inputs are finite; a program needn't handle non-finite values.
Results may differ from a plain program's by a relative error of at most 0.0044.
Values may be sent and summed in bfloat16 or wider, within the bound.
No kernel may reach another device: no remote copies, remote signals or barrier semaphores. Data moves between devices by JAX's collectives and lax.ppermute only.
A program may use at most 128 MiB of HBM per device.

v0:
```python
import functools
import math

import jax
import jax.numpy as jnp
from jax import lax
from jax.experimental import pallas as pl
from jax.experimental.pallas import tpu as pltpu
from jax.sharding import PartitionSpec as P


NBF = 128
META = 8
LINE = 32
POOL = 16
AXES = ("gx", "gy")
HI = lax.Precision.HIGHEST


def any_spec():
    return pl.BlockSpec(memory_space=pl.ANY)


def smem_spec():
    return pl.BlockSpec(memory_space=pltpu.SMEM)


def vmem_spec():
    return pl.BlockSpec(memory_space=pltpu.VMEM)


def block_rows(rank):
    return pl.ds(pl.multiple_of(rank * NBF, NBF), NBF)


def panel(ranks):
    return jax.ShapeDtypeStruct((ranks * NBF + META, NBF), jnp.bfloat16)


def ranks_of(array):
    return array.shape[-2] // NBF


def meta_rows(array):
    return pl.ds(ranks_of(array) * NBF, META)


def lane_row(shape):
    lane = lax.broadcasted_iota(jnp.int32, shape, len(shape) - 1)
    row = lax.broadcasted_iota(jnp.int32, shape, len(shape) - 2)
    return lane, row


def plan_kernel(dest, code, heads, places, count, codes, codes16, sem):
    copies, owned = dest.shape
    domains = heads.shape[0]

    @pl.loop(0, domains)
    def _(d):
        count[d] = 0

    codes[...] = jnp.full(codes.shape, -1.0, jnp.float32)
    lane, row = lane_row((META, NBF))

    @pl.loop(0, owned)
    def _(p):
        for t in range(copies):
            d = dest[t, p]
            rank = count[d]
            count[d] = rank + 1
            places[t, p] = d * LINE + rank
            value = code[t, p].astype(jnp.float32)
            codes[d] = jnp.where((lane == rank) & (row == 0), value, codes[d])

    codes16[...] = codes[...].astype(jnp.bfloat16)
    copy = pltpu.make_async_copy(codes16, heads, sem)
    copy.start()
    copy.wait()


def plan_blocks(dest, code, domains):
    owned, copies = dest.shape
    return pl.pallas_call(
        plan_kernel,
        out_shape=(
            jax.ShapeDtypeStruct((domains, META, NBF), jnp.bfloat16),
            jax.ShapeDtypeStruct((copies, owned), jnp.int32),
        ),
        in_specs=[smem_spec(), smem_spec()],
        out_specs=(any_spec(), smem_spec()),
        scratch_shapes=[
            pltpu.SMEM((domains,), jnp.int32),
            pltpu.VMEM((domains, META, NBF), jnp.float32),
            pltpu.VMEM((domains, META, NBF), jnp.bfloat16),
            pltpu.SemaphoreType.DMA,
        ],
        name="plan_blocks",
    )(dest.T, code.T)


def split_kernel(direct, groups, dest, code, density, *refs):
    copies, owned = dest.shape
    rows_x, rows_z = groups
    domains = rows_x * rows_z
    shift = rows_z.bit_length() - 1
    *panels, places = refs[:-7]
    count, pool, table, blocks, ints, codes16, sems = refs[-7:]
    load = pltpu.make_async_copy(density, blocks, sems.at[0])
    load.start()
    ints[...] = jnp.full(ints.shape, -1, jnp.int32)
    fill = pltpu.make_async_copy(ints, table, sems.at[1])
    fill.start()

    @pl.loop(0, domains)
    def _(d):
        count[d] = 0

    for k in range(rows_z + 2):
        pool[k] = 0
    live, over = rows_z, rows_z + 1
    me_x, me_z = lax.axis_index("gx"), lax.axis_index("gy")
    fill.wait()
    load.wait()

    @pl.loop(0, owned)
    def _(p):
        for t in range(copies):
            d = dest[t, p]
            value = code[t, p]
            rank = count[d]
            count[d] = rank + 1
            target = d >> shift
            near = target ^ me_x
            far = (d & (rows_z - 1)) ^ me_z
            places[t, p] = d * LINE + rank

            @pl.when((rank < direct) & (far == 0))
            def _():
                table[near, 1, rank] = value

            @pl.when((rank < direct) & (far != 0))
            def _():
                table[rows_x + far - 1, 2, target * direct + rank] = value

            @pl.when((rank >= direct) & (far == 0))
            def _():
                slot = rank - direct
                table[near, 0, slot] = value
                places[t, p] = (domains + near) * LINE + slot
                pool[live] = pool[live] + 1
                for k in range(rows_x):

                    @pl.when(near == k)
                    def _():
                        pltpu.make_async_copy(blocks.at[p], panels[k].at[block_rows(slot)], sems.at[2]).start()

            @pl.when((rank >= direct) & (far != 0))
            def _():
                taken = pool[far]
                pool[far] = taken + 1
                pool[over] = pool[over] | (taken >= POOL).astype(jnp.int32)
                slot = jnp.minimum(taken, POOL - 1)
                table[rows_x + far - 1, 0, slot] = value
                table[rows_x + far - 1, 1, slot] = target
                places[t, p] = (domains + rows_x + far - 1) * LINE + slot
                pool[live] = pool[live] + 1
                for k in range(1, rows_z):

                    @pl.when(far == k)
                    def _():
                        ref = panels[rows_x + k - 1]
                        pltpu.make_async_copy(blocks.at[p], ref.at[block_rows(slot)], sems.at[2]).start()

    for k in range(len(panels)):
        table[k, 3, 0] = pool[over]
    back = pltpu.make_async_copy(table, ints, sems.at[1])
    back.start()
    back.wait()
    codes16[...] = ints[...].astype(jnp.float32).astype(jnp.bfloat16)
    metas = [
        pltpu.make_async_copy(codes16.at[k], ref.at[meta_rows(ref), :], sems.at[3 + k]) for k, ref in enumerate(panels)
    ]
    for copy in metas:
        copy.start()

    @pl.loop(0, pool[live])
    def _(k):
        pltpu.make_async_copy(blocks.at[0], panels[0].at[block_rows(0)], sems.at[2]).wait()

    for copy in metas:
        copy.wait()


def split_blocks(density, dest, code, direct, groups):
    owned, copies = dest.shape
    panels = [panel(direct)] * groups[0] + [panel(POOL)] * (groups[1] - 1)
    return pl.pallas_call(
        functools.partial(split_kernel, direct, groups),
        out_shape=(*panels, jax.ShapeDtypeStruct((copies, owned), jnp.int32)),
        in_specs=[smem_spec(), smem_spec(), any_spec()],
        out_specs=(any_spec(),) * len(panels) + (smem_spec(),),
        scratch_shapes=[
            pltpu.SMEM((groups[0] * groups[1],), jnp.int32),
            pltpu.SMEM((LINE,), jnp.int32),
            pltpu.SMEM((len(panels), META, NBF), jnp.int32),
            pltpu.VMEM((owned, NBF, NBF), jnp.bfloat16),
            pltpu.VMEM((len(panels), META, NBF), jnp.int32),
            pltpu.VMEM((len(panels), META, NBF), jnp.bfloat16),
            pltpu.SemaphoreType.DMA((3 + len(panels),)),
        ],
        name="split_blocks",
    )(dest.T, code.T, density)


def direct_kernel(places, density, out, blocks, live, load_sem, out_sem):
    copies, owned = places.shape
    domains = out.shape[0]
    load = pltpu.make_async_copy(density, blocks, load_sem)
    load.start()
    load.wait()
    live[0] = 0

    @pl.loop(0, owned)
    def _(p):
        for t in range(copies):
            entry = places[t, p] // LINE
            rows = block_rows(places[t, p] - entry * LINE)

            @pl.when(entry < domains)
            def _():
                live[0] = live[0] + 1
                pltpu.make_async_copy(blocks.at[p], out.at[entry, rows], out_sem).start()

    @pl.loop(0, live[0])
    def _(k):
        pltpu.make_async_copy(blocks.at[0], out.at[0, block_rows(0)], out_sem).wait()


def direct_blocks(places, density, domains, direct):
    return pl.pallas_call(
        direct_kernel,
        out_shape=jax.ShapeDtypeStruct((domains, direct * NBF, NBF), jnp.bfloat16),
        in_specs=[smem_spec(), any_spec()],
        out_specs=any_spec(),
        scratch_shapes=[
            pltpu.VMEM(density.shape, jnp.bfloat16),
            pltpu.SMEM((1,), jnp.int32),
            pltpu.SemaphoreType.DMA,
            pltpu.SemaphoreType.DMA,
        ],
        cost_estimate=pl.CostEstimate(flops=1000, bytes_accessed=8 << 20, transcendentals=0),
        name="direct_blocks",
    )(places, density)


def scan_kernel(direct, heads, *refs):
    extras = refs[:-9]
    starts, places, marks, lines, codes_v, codes, live, line_sem, code_sem = refs[-9:]
    sources = heads.shape[0]
    loads = [pltpu.make_async_copy(heads, lines.at[pl.ds(0, sources)], line_sem.at[0])]
    for k, ref in enumerate(extras):
        loads.append(pltpu.make_async_copy(ref.at[meta_rows(ref), :], lines.at[sources + k], line_sem.at[1 + k]))
    for load in loads:
        load.start()
    for load in loads:
        load.wait()
    head = lax.broadcasted_iota(jnp.int32, lines.shape, 1) == 0
    codes_v[...] = jnp.sum(jnp.where(head, lines[...].astype(jnp.float32), 0.0), axis=1).astype(jnp.int32)
    load = pltpu.make_async_copy(codes_v, codes, code_sem)
    load.start()
    load.wait()
    live[0] = 0

    def note(entry, rank):
        c = codes[entry, rank]

        @pl.when(c >= 0)
        def _():
            k = live[0]
            places[k] = entry * LINE + rank
            marks[k] = c
            live[0] = k + 1

    starts[0] = 0

    @pl.loop(0, sources)
    def _(source):
        for rank in range(direct):
            note(source, rank)

    starts[1] = live[0]
    for k, ref in enumerate(extras):

        @pl.loop(0, ranks_of(ref))
        def _(rank):
            note(sources + k, rank)

        starts[2 + k] = live[0]


def scan(heads, extras, direct):
    sources = heads.shape[0]
    entries = sources + len(extras)
    slots = sources * direct + sum(ranks_of(ref) for ref in extras)
    return pl.pallas_call(
        functools.partial(scan_kernel, direct),
        out_shape=(
            jax.ShapeDtypeStruct((2 + len(extras),), jnp.int32),
            jax.ShapeDtypeStruct((slots,), jnp.int32),
            jax.ShapeDtypeStruct((slots,), jnp.int32),
        ),
        in_specs=[any_spec()] * (1 + len(extras)),
        out_specs=(smem_spec(),) * 3,
        scratch_shapes=[
            pltpu.VMEM((entries, META, NBF), jnp.bfloat16),
            pltpu.VMEM((entries, NBF), jnp.int32),
            pltpu.SMEM((entries, NBF), jnp.int32),
            pltpu.SMEM((1,), jnp.int32),
            pltpu.SemaphoreType.DMA((1 + len(extras),)),
            pltpu.SemaphoreType.DMA,
        ],
        cost_estimate=pl.CostEstimate(flops=1000, bytes_accessed=8 << 20, transcendentals=0),
        name="scan",
    )(heads, *extras)


def merge_kernel(direct, groups, *refs):
    rows_x, rows_z = groups
    panels = refs[:-9]
    starts, places, marks, raised, lines, ints, info, live, sems = refs[-9:]
    loads = [pltpu.make_async_copy(ref.at[meta_rows(ref), :], lines.at[k], sems.at[k]) for k, ref in enumerate(panels)]
    for load in loads:
        load.start()
    for load in loads:
        load.wait()
    ints[...] = lines[...].astype(jnp.float32).astype(jnp.int32)
    load = pltpu.make_async_copy(ints, info, sems.at[0])
    load.start()
    load.wait()
    me_x, me_z = lax.axis_index("gx"), lax.axis_index("gy")
    live[0] = 0
    raised[0] = 0
    starts[0] = 0

    def note(entry, rank, c):
        @pl.when(c >= 0)
        def _():
            k = live[0]
            places[k] = entry * LINE + rank
            marks[k] = c
            live[0] = k + 1

    @pl.loop(0, rows_x)
    def _(k):
        first = (k ^ me_x) * rows_z
        raised[0] = raised[0] | info[k, 3, 0] | info[rows_x + k, 3, 0]
        for rank in range(direct):
            note(first + me_z, rank, info[k, 1, rank])
            for h in range(rows_z - 1):
                note(first + (me_z ^ (h + 1)), rank, info[rows_x + k, 1, h * direct + rank])

    starts[1] = live[0]
    domains = rows_x * rows_z
    for k, ref in enumerate(panels):

        @pl.loop(0, ranks_of(ref))
        def _(rank):
            note(domains + k, rank, info[k, 0, rank])

        starts[2 + k] = live[0]


def merge(panels, direct, groups):
    slots = groups[0] * groups[1] * direct + sum(ranks_of(ref) for ref in panels)
    return pl.pallas_call(
        functools.partial(merge_kernel, direct, groups),
        out_shape=(
            jax.ShapeDtypeStruct((2 + len(panels),), jnp.int32),
            jax.ShapeDtypeStruct((slots,), jnp.int32),
            jax.ShapeDtypeStruct((slots,), jnp.int32),
            jax.ShapeDtypeStruct((1,), jnp.int32),
        ),
        in_specs=[any_spec()] * len(panels),
        out_specs=(smem_spec(),) * 4,
        scratch_shapes=[
            pltpu.VMEM((len(panels), META, NBF), jnp.bfloat16),
            pltpu.VMEM((len(panels), META, NBF), jnp.int32),
            pltpu.SMEM((len(panels), META, NBF), jnp.int32),
            pltpu.SMEM((1,), jnp.int32),
            pltpu.SemaphoreType.DMA((len(panels),)),
        ],
        cost_estimate=pl.CostEstimate(flops=1000, bytes_accessed=8 << 20, transcendentals=0),
        name="merge",
    )(*panels)


def relay_kernel(direct, *refs):
    info, count, table, stage, lines, ints, cells, codes16, in_sem, sems = refs[-10:]
    hops = lines.shape[0]
    arrived = refs[:hops]
    outs = refs[hops:-11]
    places = refs[-11]
    ranks = ranks_of(outs[0])
    me = lax.axis_index("gx")
    loads = [
        pltpu.make_async_copy(ref.at[meta_rows(ref), :], lines.at[h], sems.at[h]) for h, ref in enumerate(arrived)
    ]
    for load in loads:
        load.start()
    last = sems.at[hops + len(outs)]
    cells[...] = jnp.full(cells.shape, -1, jnp.int32)
    fill = pltpu.make_async_copy(cells, table, last)
    fill.start()
    for k in range(len(outs)):
        count[k] = 0
    for load in loads:
        load.wait()
    ints[...] = lines[...].astype(jnp.float32).astype(jnp.int32)
    load = pltpu.make_async_copy(ints, info, sems.at[0])
    load.start()
    load.wait()
    fill.wait()

    def fetch(h, q):
        return pltpu.make_async_copy(arrived[h].at[block_rows(q)], stage.at[h * POOL + q], in_sem.at[h * POOL + q])

    for h in range(hops):

        @pl.loop(0, POOL)
        def _(q):
            places[h, q] = -1
            c = info[h, 0, q]

            @pl.when(c >= 0)
            def _():
                fetch(h, q).start()
                near = info[h, 1, q] ^ me
                slot = jnp.minimum(count[near], ranks - 1)
                count[near] = slot + 1
                places[h, q] = near * LINE + slot
                table[near, 0, slot] = c

    raised = functools.reduce(jnp.bitwise_or, [info[h, 3, 0] for h in range(hops)])

    @pl.loop(0, len(outs))
    def _(k):
        table[k, 3, 0] = raised
        for h in range(hops):
            for rank in range(direct):
                table[k, 1, h * direct + rank] = info[h, 2, (k ^ me) * direct + rank]

    back = pltpu.make_async_copy(table, cells, last)
    back.start()
    back.wait()
    codes16[...] = cells[...].astype(jnp.float32).astype(jnp.bfloat16)
    metas = [
        pltpu.make_async_copy(codes16.at[k], ref.at[meta_rows(ref), :], sems.at[hops + k])
        for k, ref in enumerate(outs)
    ]
    for copy in metas:
        copy.start()
    for h in range(hops):

        @pl.loop(0, POOL)
        def _(q):
            place = places[h, q]

            @pl.when(place >= 0)
            def _():
                fetch(h, q).wait()
                near = place // LINE
                rows = block_rows(place - near * LINE)
                for k, ref in enumerate(outs):

                    @pl.when(near == k)
                    def _():
                        pltpu.make_async_copy(stage.at[h * POOL + q], ref.at[rows], last).start()

    for copy in metas:
        copy.wait()
    for h in range(hops):

        @pl.loop(0, POOL)
        def _(q):
            @pl.when(places[h, q] >= 0)
            def _():
                pltpu.make_async_copy(stage.at[0], outs[0].at[block_rows(0)], last).wait()


def relay(arrived, near_count, ranks, direct):
    hops = len(arrived)
    return pl.pallas_call(
        functools.partial(relay_kernel, direct),
        out_shape=tuple([panel(ranks)] * near_count + [jax.ShapeDtypeStruct((hops, POOL), jnp.int32)]),
        in_specs=[any_spec()] * hops,
        out_specs=tuple([any_spec()] * near_count + [smem_spec()]),
        scratch_shapes=[
            pltpu.SMEM((hops, META, NBF), jnp.int32),
            pltpu.SMEM((near_count,), jnp.int32),
            pltpu.SMEM((near_count, META, NBF), jnp.int32),
            pltpu.VMEM((hops * POOL, NBF, NBF), jnp.bfloat16),
            pltpu.VMEM((hops, META, NBF), jnp.bfloat16),
            pltpu.VMEM((hops, META, NBF), jnp.int32),
            pltpu.VMEM((near_count, META, NBF), jnp.int32),
            pltpu.VMEM((near_count, META, NBF), jnp.bfloat16),
            pltpu.SemaphoreType.DMA((hops * POOL,)),
            pltpu.SemaphoreType.DMA((hops + near_count + 1,)),
        ],
        cost_estimate=pl.CostEstimate(flops=1000, bytes_accessed=4 << 20, transcendentals=0),
        name="relay",
    )(*arrived)


def relay_back_kernel(places, *refs):
    stage, in_sem, out_sem = refs[-3:]
    hops = places.shape[0]
    arrived, outs = refs[: -3 - hops], refs[-3 - hops : -3]

    def fetch(ref, rows, h, q):
        return pltpu.make_async_copy(ref.at[rows], stage.at[h * POOL + q], in_sem.at[h * POOL + q])

    def give(h, q):
        return pltpu.make_async_copy(stage.at[h * POOL + q], outs[h].at[block_rows(q)], out_sem)

    for h in range(hops):

        @pl.loop(0, POOL)
        def _(q):
            place = places[h, q]

            @pl.when(place >= 0)
            def _():
                near = place // LINE
                rows = block_rows(place - near * LINE)
                for k, ref in enumerate(arrived):

                    @pl.when(near == k)
                    def _():
                        fetch(ref, rows, h, q).start()

    for h in range(hops):

        @pl.loop(0, POOL)
        def _(q):
            @pl.when(places[h, q] >= 0)
            def _():
                fetch(arrived[0], block_rows(0), h, q).wait()
                give(h, q).start()

    for h in range(hops):

        @pl.loop(0, POOL)
        def _(q):
            @pl.when(places[h, q] >= 0)
            def _():
                give(h, q).wait()


def relay_back(places, arrived):
    hops = places.shape[0]
    return pl.pallas_call(
        relay_back_kernel,
        out_shape=tuple([panel(POOL)] * hops),
        in_specs=[smem_spec()] + [any_spec()] * len(arrived),
        out_specs=tuple([any_spec()] * hops),
        scratch_shapes=[
            pltpu.VMEM((hops * POOL, NBF, NBF), jnp.bfloat16),
            pltpu.SemaphoreType.DMA((hops * POOL,)),
            pltpu.SemaphoreType.DMA,
        ],
        cost_estimate=pl.CostEstimate(flops=1000, bytes_accessed=4 << 20, transcendentals=0),
        name="relay_back",
    )(places, *arrived)


def domain_kernel(extra_count, starts, places, marks, *refs):
    inbound, *extras = refs[: 1 + extra_count]
    basis, basis_t, base_in, w_in, w_hid1, w_hid1_t, w_hid2, w_hid2_t, w_last, weights = refs[
        1 + extra_count : 11 + extra_count
    ]
    reply, *extra_replies = refs[11 + extra_count : 12 + 2 * extra_count]
    (
        seen,
        stage,
        acc,
        dense,
        basis_v,
        basis_tv,
        rho,
        hid1,
        hid2,
        blocks,
        meta,
        w_row,
        w_out,
        in_sem,
        basis_sem,
        out_sem,
        meta_sem,
    ) = refs[12 + 2 * extra_count :]
    sources = inbound.shape[0]
    direct = ranks_of(inbound)
    points, order = basis.shape
    width = order // NBF
    pairs = width * width
    load_t = pltpu.make_async_copy(basis_t, basis_tv, basis_sem.at[0])
    load_n = pltpu.make_async_copy(basis, basis_v, basis_sem.at[1])
    live = starts[1 + extra_count]

    @pl.loop(0, starts[1])
    def _(k):
        entry = places[k] // LINE
        rows = block_rows(places[k] - entry * LINE)
        pltpu.make_async_copy(inbound.at[entry, rows], stage.at[k], in_sem.at[k]).start()

    for e, ref in enumerate(extras):

        @pl.loop(starts[1 + e], starts[2 + e])
        def _(k):
            rows = block_rows(places[k] - (sources + e) * LINE)
            pltpu.make_async_copy(ref.at[rows], stage.at[k], in_sem.at[k]).start()

    load_t.start()
    load_n.start()

    @pl.loop(0, pairs)
    def _(c):
        seen[c] = 0

    w_row[...] = jnp.broadcast_to(w_in[0:1, :], w_row.shape).T
    w_out[...] = jnp.broadcast_to(w_last[...], w_out.shape).T

    @pl.loop(0, live)
    def _(k):
        c = marks[k]
        pltpu.make_async_copy(inbound.at[0, block_rows(0)], stage.at[k], in_sem.at[k]).wait()
        value = stage[k].astype(jnp.float32)
        before = seen[c]
        seen[c] = 1

        @pl.when(before == 0)
        def _():
            acc[c] = value

        @pl.when(before != 0)
        def _():
            acc[c] = acc[c] + value

    @pl.loop(0, width)
    def _(a):
        rows = block_rows(a)
        for b in range(width):
            there = seen[a * width + b] != 0
            value = jnp.where(there, acc[a * width + b], 0.0)
            dense[rows, b * NBF : (b + 1) * NBF] = value.astype(jnp.bfloat16)

    load_t.wait()
    tile = 512

    @pl.loop(0, points // tile)
    def _(n):
        cols = pl.ds(pl.multiple_of(n * tile, tile), tile)
        part = basis_tv[:, cols]
        projected = jnp.dot(dense[...], part, preferred_element_type=jnp.float32)
        rho[:, cols] = jnp.sum(projected * part.astype(jnp.float32), axis=0, keepdims=True)

    h1 = jnp.tanh(base_in[...] + w_row[:, 0:1] * rho[...])
    hid1[...] = h1
    h2 = jnp.tanh(jnp.dot(w_hid1_t[...], h1, precision=HI, preferred_element_type=jnp.float32))
    hid2[...] = h2
    h3 = jnp.tanh(jnp.dot(w_hid2_t[...], h2, precision=HI, preferred_element_type=jnp.float32))
    logits = jnp.sum(w_out[:, 0:1] * h3, axis=0, keepdims=True)
    decay = jnp.exp(-jnp.abs(logits))
    energy_at = -(jnp.maximum(logits, 0.0) + jnp.log1p(decay))
    slope = -jnp.where(logits >= 0, 1.0, decay) / (1.0 + decay)
    g3 = (w_out[:, 0:1] * slope) * (1.0 - h3 * h3)
    h2 = hid2[...]
    g2 = jnp.dot(w_hid2[...], g3, precision=HI, preferred_element_type=jnp.float32) * (1.0 - h2 * h2)
    h1 = hid1[...]
    g1 = jnp.dot(w_hid1[...], g2, precision=HI, preferred_element_type=jnp.float32) * (1.0 - h1 * h1)
    deriv = jnp.sum(w_row[:, 0:1] * g1, axis=0, keepdims=True)
    rho[...] = weights[...] * deriv
    total = jnp.sum(weights[...] * energy_at, axis=1, keepdims=True)
    top = total.astype(jnp.bfloat16).astype(jnp.float32)
    rest = total - top
    middle = rest.astype(jnp.bfloat16).astype(jnp.float32)
    low = rest - middle
    lane = lax.broadcasted_iota(jnp.int32, (META, NBF), 1)
    line = jnp.where(lane == 0, top, jnp.where(lane == 1, middle, jnp.where(lane == 2, low, 0.0)))
    meta[...] = line.astype(jnp.bfloat16)

    @pl.loop(0, sources)
    def _(source):
        pltpu.make_async_copy(meta, reply.at[source, pl.ds(direct * NBF, META)], meta_sem).start()

    load_n.wait()

    @pl.loop(0, points // NBF)
    def _(n):
        rows = block_rows(n)
        line = jnp.broadcast_to(rho[:, rows], (NBF, NBF))
        column = line.T
        for b in range(width):
            cols = slice(b * NBF, (b + 1) * NBF)
            basis_v[rows, cols] = (column * basis_v[rows, cols].astype(jnp.float32)).astype(jnp.bfloat16)

    @pl.loop(0, width // 2)
    def _(n):
        cols = pl.ds(pl.multiple_of(n * 2 * NBF, 2 * NBF), 2 * NBF)
        result = jnp.dot(basis_tv[...], basis_v[:, cols], preferred_element_type=jnp.float32).astype(jnp.bfloat16)
        for a in range(width):
            for half in range(2):
                blocks[a * width + 2 * n + half] = result[a * NBF : (a + 1) * NBF, half * NBF : (half + 1) * NBF]

    def give(ref, rows, k):
        pltpu.make_async_copy(blocks.at[marks[k]], ref.at[rows], out_sem).start()

    for e, ref in enumerate(extra_replies):

        @pl.loop(starts[1 + e], starts[2 + e])
        def _(k):
            give(ref, block_rows(places[k] - (sources + e) * LINE), k)

    @pl.loop(0, starts[1])
    def _(k):
        entry = places[k] // LINE
        give(reply.at[entry], block_rows(places[k] - entry * LINE), k)

    @pl.loop(0, live)
    def _(k):
        pltpu.make_async_copy(blocks.at[0], reply.at[0, block_rows(0)], out_sem).wait()

    whole = reply.at[:, meta_rows(reply), :]
    pltpu.make_async_copy(whole, whole, meta_sem).wait()


def domain_build(lists, inbound, extras, basis, *fixed):
    sources = inbound.shape[0]
    direct = ranks_of(inbound)
    points, order = basis.shape
    hid = fixed[1].shape[0]
    pairs = (order // NBF) ** 2
    slots = lists[1].shape[0]
    arrays = [inbound] + list(extras)
    replies = [jax.ShapeDtypeStruct((sources, direct * NBF + META, NBF), jnp.bfloat16)]
    replies += [jax.ShapeDtypeStruct((ranks_of(ref) * NBF, NBF), jnp.bfloat16) for ref in extras]
    return pl.pallas_call(
        functools.partial(domain_kernel, len(extras)),
        out_shape=tuple(replies),
        in_specs=[smem_spec()] * 3 + [any_spec()] * (len(arrays) + 2) + [vmem_spec()] * 8,
        out_specs=(any_spec(),) * len(arrays),
        scratch_shapes=[
            pltpu.SMEM((pairs,), jnp.int32),
            pltpu.VMEM((slots, NBF, NBF), jnp.bfloat16),
            pltpu.VMEM((pairs, NBF, NBF), jnp.float32),
            pltpu.VMEM((order, order), jnp.bfloat16),
            pltpu.VMEM((points, order), jnp.bfloat16),
            pltpu.VMEM((order, points), jnp.bfloat16),
            pltpu.VMEM((1, points), jnp.float32),
            pltpu.VMEM((hid, points), jnp.float32),
            pltpu.VMEM((hid, points), jnp.float32),
            pltpu.VMEM((pairs, NBF, NBF), jnp.bfloat16),
            pltpu.VMEM((META, NBF), jnp.bfloat16),
            pltpu.VMEM((NBF, hid), jnp.float32),
            pltpu.VMEM((NBF, hid), jnp.float32),
            pltpu.SemaphoreType.DMA((slots,)),
            pltpu.SemaphoreType.DMA((2,)),
            pltpu.SemaphoreType.DMA,
            pltpu.SemaphoreType.DMA,
        ],
        compiler_params=pltpu.CompilerParams(vmem_limit_bytes=60 << 20),
        name="domain_build",
    )(*lists, *arrays, basis, *fixed)


def collect_kernel(scale, places, returned, *refs):
    extras = refs[:-8]
    fock, energy, parts, result, meta, in_sem, out_sem, meta_sem = refs[-8:]
    copies, owned = places.shape
    sources = returned.shape[0]
    meta_in = pltpu.make_async_copy(returned.at[:, meta_rows(returned), :], meta, meta_sem)
    meta_in.start()

    @pl.loop(0, owned)
    def _(p):
        for t in range(copies):
            entry = places[t, p] // LINE
            rows = block_rows(places[t, p] - entry * LINE)

            @pl.when(entry < sources)
            def _():
                pltpu.make_async_copy(returned.at[entry, rows], parts.at[p, t], in_sem.at[p]).start()

            if extras:

                @pl.when(entry >= sources)
                def _():
                    for k, ref in enumerate(extras):

                        @pl.when(entry == sources + k)
                        def _():
                            pltpu.make_async_copy(ref.at[rows], parts.at[p, t], in_sem.at[p]).start()

    meta_in.wait()
    lane = lax.broadcasted_iota(jnp.int32, meta.shape, 2)
    row = lax.broadcasted_iota(jnp.int32, meta.shape, 1)
    sent = jnp.where((lane < 3) & (row == 0), meta[...].astype(jnp.float32), 0.0)
    per_source = jnp.sum(jnp.sum(sent, axis=0), axis=0, keepdims=True)
    energy[...] = jnp.sum(per_source, axis=1, keepdims=True) * scale
    last = (sources + len(extras)) * LINE

    @pl.loop(0, owned)
    def _(p):
        total = jnp.zeros((NBF, NBF), jnp.float32)
        for t in range(copies):
            here = places[t, p] < last

            @pl.when(here)
            def _():
                pltpu.make_async_copy(parts.at[p, t], parts.at[p, t], in_sem.at[p]).wait()

            total = total + jnp.where(here, parts[p, t].astype(jnp.float32), 0.0)
        result[p] = total
        pltpu.make_async_copy(result.at[p], fock.at[p], out_sem).start()

    pltpu.make_async_copy(result, fock, out_sem).wait()


def collect_blocks(places, returned, extras, scale):
    copies, owned = places.shape
    sources = returned.shape[0]
    return pl.pallas_call(
        functools.partial(collect_kernel, scale),
        out_shape=(
            jax.ShapeDtypeStruct((owned, NBF, NBF), jnp.float32),
            jax.ShapeDtypeStruct((1, 1), jnp.float32),
        ),
        in_specs=[smem_spec()] + [any_spec()] * (1 + len(extras)),
        out_specs=(any_spec(), vmem_spec()),
        scratch_shapes=[
            pltpu.VMEM((owned, copies, NBF, NBF), jnp.bfloat16),
            pltpu.VMEM((owned, NBF, NBF), jnp.float32),
            pltpu.VMEM((sources, META, NBF), jnp.bfloat16),
            pltpu.SemaphoreType.DMA((owned,)),
            pltpu.SemaphoreType.DMA,
            pltpu.SemaphoreType.DMA,
        ],
        cost_estimate=pl.CostEstimate(flops=1000, bytes_accessed=8 << 20, transcendentals=0),
        name="collect_blocks",
    )(places, returned, *extras)


def add_kernel(first, places, partial, *refs):
    extras = refs[:-8]
    fock, parts, result, listed, live, in_sem, fock_sem, out_sem = refs[-8:]
    copies, owned = places.shape
    live[0] = 0

    @pl.loop(0, owned)
    def _(p):
        hits = [places[t, p] >= first * LINE for t in range(copies)]

        @pl.when(functools.reduce(jnp.logical_or, hits))
        def _():
            k = live[0]
            listed[k] = p
            live[0] = k + 1
            pltpu.make_async_copy(partial.at[p], result.at[k], fock_sem.at[k]).start()
            for t in range(copies):
                entry = places[t, p] // LINE
                rows = block_rows(places[t, p] - entry * LINE)
                for e, ref in enumerate(extras):

                    @pl.when(entry == first + e)
                    def _():
                        pltpu.make_async_copy(ref.at[rows], parts.at[k, t], in_sem.at[k]).start()

    @pl.loop(0, live[0])
    def _(k):
        p = listed[k]
        pltpu.make_async_copy(partial.at[p], result.at[k], fock_sem.at[k]).wait()
        total = result[k]
        for t in range(copies):
            here = places[t, p] >= first * LINE

            @pl.when(here)
            def _():
                pltpu.make_async_copy(parts.at[k, t], parts.at[k, t], in_sem.at[k]).wait()

            total = total + jnp.where(here, parts[k, t].astype(jnp.float32), 0.0)
        result[k] = total
        pltpu.make_async_copy(result.at[k], fock.at[p], out_sem).start()

    @pl.loop(0, live[0])
    def _(k):
        pltpu.make_async_copy(result.at[0], fock.at[0], out_sem).wait()


def add_blocks(places, partial, extras, first):
    copies, owned = places.shape
    return pl.pallas_call(
        functools.partial(add_kernel, first),
        out_shape=jax.ShapeDtypeStruct(partial.shape, partial.dtype),
        in_specs=[smem_spec()] + [any_spec()] * (1 + len(extras)),
        out_specs=any_spec(),
        input_output_aliases={1: 0},
        scratch_shapes=[
            pltpu.VMEM((owned, copies, NBF, NBF), jnp.bfloat16),
            pltpu.VMEM((owned, NBF, NBF), jnp.float32),
            pltpu.SMEM((owned,), jnp.int32),
            pltpu.SMEM((1,), jnp.int32),
            pltpu.SemaphoreType.DMA((owned,)),
            pltpu.SemaphoreType.DMA((owned,)),
            pltpu.SemaphoreType.DMA,
        ],
        name="add_blocks",
    )(places, partial, *extras)


def exchange(array):
    return lax.all_to_all(array, AXES, split_axis=0, concat_axis=0, tiled=True)


def swap(arrays, axis, first):
    size = lax.axis_size(axis)
    return [
        lax.ppermute(array, axis, [(i, i ^ (first + k)) for i in range(size)]) if first + k else array
        for k, array in enumerate(arrays)
    ]


def body(density, dest, code, basis, descriptors, weights, w_in, w_hid1, w_hid2, w_out):
    rows_x, rows_z = lax.axis_size("gx"), lax.axis_size("gy")
    domains = rows_x * rows_z
    owned = density.shape[0]
    copies = dest.shape[1]
    capacity = max(2, 2 * copies * owned // domains)
    points = basis.shape[0]
    scale = 1.0 / (math.sqrt(points) * domains)
    basis_t = basis.T
    base_in = jnp.dot(w_in[1:].T, descriptors, precision=HI)
    fixed = (
        basis, basis_t, base_in, w_in, w_hid1, w_hid1.T, w_hid2, w_hid2.T, w_out[None, :], weights[None, :]
    )

    def plain():
        heads, places = plan_blocks(dest, code, domains)
        lists = scan(exchange(heads), [], capacity)
        inbound = exchange(direct_blocks(places, density, domains, capacity))
        (replies,) = domain_build(lists, inbound, [], *fixed)
        fock, energy = collect_blocks(places, exchange(replies), [], scale)
        return fock, energy[0, 0]

    if capacity < 8:
        return plain()
    direct = capacity // 2
    ranks = (rows_z - 1) * (capacity - direct)
    groups = (rows_x, rows_z)
    *panels, places = split_blocks(density, dest, code, direct, groups)
    lines_in = swap(panels[rows_x:], "gy", 1)
    near_in = swap(panels[:rows_x], "gx", 0)
    outgoing = direct_blocks(places, density, domains, direct)
    inbound = exchange(outgoing)
    *relayed, relay_places = relay(lines_in, rows_x, ranks, direct)
    relayed_in = swap(relayed, "gx", 0)
    *lists, raised = merge(near_in + relayed_in, direct, groups)

    def split():
        replies, *others = domain_build(lists, inbound, near_in + relayed_in, *fixed)
        relayed_back = swap(others[rows_x:], "gx", 0)
        near_back = swap(others[:rows_x], "gx", 0)
        returned = exchange(replies)
        lines_back = swap(relay_back(relay_places, relayed_back), "gy", 1)
        fock, energy = collect_blocks(places, returned, near_back, scale)
        return add_blocks(places, fock, lines_back, domains + rows_x), energy[0, 0]

    return lax.cond(raised[0] > 0, plain, split)


def solution(mesh):
    placed = (
        P(AXES, None, None),
        P(AXES, None),
        P(AXES, None),
        P(AXES, None),
        P(None, AXES),
        P(AXES),
        P(),
        P(),
        P(),
        P(),
    )
    return jax.shard_map(
        body,
        mesh=mesh,
        in_specs=placed,
        out_specs=(P(AXES, None, None), P()),
        check_vma=False,
    )
```

profile of v0, /device:TPU:8, one launch (start us, length us, event | category | flops | bytes accessed | tf_op | source)
XLA Modules:
  0.0 436.1 jit_solution(13426823394995418231)
XLA Ops:
  0.6 11.0 %split_blocks.1 = (bf16[520,128]{1,0:T(8,128)(2,1)}, bf16[520,128]{1,0:T(8,128)(2,1)}, bf16[520,128]{1,0:T(8,128)(2,1)}, bf16[520,128]{1,0:T(8,128)(2,1)}, bf16[...) custom-call(s32[2,64]{1,0:T(2,128)} %bitcast.21, ...), custom_call_target="tpu_custom_call" | custom-call | tf_op jit(solution)/shard_map/split_blocks/pallas_call | solution.py:197
  11.7 4.0 direct_blocks.3
  15.7 6.1 %all-to-all-start.4 = ((bf16[32,512,128]{2,1,0:T(8,128)(2,1)}), bf16[32,512,128]{2,1,0:T(8,128)(2,1)}, u32[]{:S(2)}, u32[]{:S(2)}) async-start(bf16[32,512,128]{2,1,0:T(8,128)(2,1)} %direct_blocks.3), calls=%async_computation.4 | async-start | bytes 8388608 | tf_op jit(solution)/shard_map/all_to_all | solution.py:921
  22.3 2.6 collective-permute-start.25
  25.4 77.9 %collective-permute-done.24.refs_0_ = bf16[2056,128]{1,0:T(8,128)(2,1)S(1)} collective-permute-done((bf16[2056,128]{1,0:T(8,128)(2,1)}, bf16[2056,128]{1,0:T(8,128)(2,1)S(1)}, u32[]{:S(2)}, u32[]{:S(2)}) %collective-permute-start.24) | collective-permute-done | bytes 526368 | tf_op jit(solution)/shard_map/ppermute | solution.py:927
  103.3 44.6 %collective-permute-done.25.refs_1_ = bf16[2056,128]{1,0:T(8,128)(2,1)S(1)} collective-permute-done((bf16[2056,128]{1,0:T(8,128)(2,1)S(1)}, bf16[2056,128]{1,0:T(8,128)(2,1)S(1)}, u32[]{:S(2)}, u32[]{:S(2)}) %collective-permute-start.25) | collective-permute-done | bytes 526368 | tf_op jit(solution)/shard_map/ppermute | solution.py:927
  147.9 13.5 %collective-permute-done.26.refs_2_ = bf16[2056,128]{1,0:T(8,128)(2,1)S(1)} collective-permute-done((bf16[2056,128]{1,0:T(8,128)(2,1)S(1)}, bf16[2056,128]{1,0:T(8,128)(2,1)S(1)}, u32[]{:S(2)}, u32[]{:S(2)}) %collective-permute-start.26) | collective-permute-done | bytes 526368 | tf_op jit(solution)/shard_map/ppermute | solution.py:927
  161.5 0.8 copy-done.14
  162.3 6.9 %relay.1 = (bf16[1544,128]{1,0:T(8,128)(2,1)}, bf16[1544,128]{1,0:T(8,128)(2,1)}, bf16[1544,128]{1,0:T(8,128)(2,1)}, bf16[1544,128]{1,0:T(8,128)(2,1)}, bf16[154...) custom-call(bf16[2056,128]{1,0:T(8,128)(2,1)} %copy-done.12, ...), custom_call_target="tpu_custom_call" | custom-call | flops 1000 | bytes 4194304 | tf_op jit(solution)/shard_map/relay/pallas_call | solution.py:492
  169.3 2.0 collective-permute-start.18
  171.4 1.6 collective-permute-start.20
  172.9 11.5 %collective-permute-done.18.refs_2_ = bf16[520,128]{1,0:T(8,128)(2,1)S(1)} collective-permute-done((bf16[520,128]{1,0:T(8,128)(2,1)}, bf16[520,128]{1,0:T(8,128)(2,1)S(1)}, u32[]{:S(2)}, u32[]{:S(2)}) %collective-permute-start.18) | collective-permute-done | bytes 133152 | tf_op jit(solution)/shard_map/ppermute | solution.py:927
  184.6 1.6 collective-permute-done.19.refs_3_
  186.2 1.5 collective-permute-start.22
  187.7 1.2 collective-permute-start.23
  188.9 6.6 %collective-permute-done.21.refs_5_ = bf16[520,128]{1,0:T(8,128)(2,1)S(1)} collective-permute-done((bf16[520,128]{1,0:T(8,128)(2,1)S(1)}, bf16[520,128]{1,0:T(8,128)(2,1)S(1)}, u32[]{:S(2)}, u32[]{:S(2)}) %collective-permute-start.21) | collective-permute-done | bytes 133152 | tf_op jit(solution)/shard_map/ppermute | solution.py:927
  195.6 1.4 collective-permute-start.31
  197.0 1.7 collective-permute-start.32
  198.8 1.2 collective-permute-start.33
  200.2 8.7 %copy.17 = bf16[2048,1536]{0,1:T(8,128)(2,1)} copy(bf16[2048,1536]{1,0:T(8,128)(2,1)} %param.15) | data formatting | bytes 12582912 | tf_op args[3]
  209.0 1.0 fusion
  210.0 14.8 %collective-permute-done.30.refs_12_ = bf16[1544,128]{1,0:T(8,128)(2,1)} collective-permute-done((bf16[1544,128]{1,0:T(8,128)(2,1)}, bf16[1544,128]{1,0:T(8,128)(2,1)}, u32[]{:S(2)}, u32[]{:S(2)}) %collective-permute-start.30) | collective-permute-done | bytes 395296 | tf_op jit(solution)/shard_map/ppermute | solution.py:927
  224.8 6.8 %collective-permute-done.31.refs_13_ = bf16[1544,128]{1,0:T(8,128)(2,1)} collective-permute-done((bf16[1544,128]{1,0:T(8,128)(2,1)}, bf16[1544,128]{1,0:T(8,128)(2,1)}, u32[]{:S(2)}, u32[]{:S(2)}) %collective-permute-start.31) | collective-permute-done | bytes 395296 | tf_op jit(solution)/shard_map/ppermute | solution.py:927
  231.6 4.9 %merge.1 = (s32[18]{0:T(128)S(1)}, s32[256]{0:T(256)S(1)}, s32[256]{0:T(256)S(1)}, s32[1]{0:T(128)}) custom-call(bf16[520,128]{1,0:T(8,128)(2,1)} %get-tuple-element.191.refs_0_, bf16[520,128]{1,0:T(8,128)(2,1)} %copy-done.5, bf16[520,128]{1,0:T(8,128)(2,1)} %copy-done.6, bf16[520,128]{1,0:T(8,128)(2,1)} %copy-done.7, bf16[520,128]{1,0:T(8,128)(2,1)} %copy-done.8, ...), custom_call_target="tpu_custom_call" | custom-call | flops 1000 | bytes 8388608 | tf_op jit(solution)/shard_map/merge/pallas_call | solution.py:375
  237.2 198.0 %conditional.1 = (f32[64,128,128]{2,1,0:T(8,128)}, f32[]{:T(128)}) conditional(s32[]{:T(128)} %bitcast.6, (s32[18]{0:T(128)S(1)}, s32[256]{0:T(256)S(1)}, s32[256]{0:T(256)S(1)}, bf16[32,512,128]{2,1,0:T(8,128)(2,1)}, bf16[520,128]{1,0:T(8,128)(2,1)}, /*index=5*/bf16[520,128]{1,0:T(8,128)(2,1)}, bf16[520,128]{1,0:T(8,128)(2,1)}, ...), branch_computations={%region_0.0_spmd, %region_1.0_spmd} | conditional | flops 3000 | bytes 73126008 | solution.py:977
  237.2 39.0 %domain_build.2 = (bf16[32,520,128]{2,1,0:T(8,128)(2,1)}, bf16[512,128]{1,0:T(8,128)(2,1)}, bf16[512,128]{1,0:T(8,128)(2,1)}, bf16[512,128]{1,0:T(8,128)(2,1)}, ...) custom-call(s32[18]{0:T(128)S(1)} %get-tuple-element.91.starts, ...), custom_call_target="tpu_custom_call" | custom-call | tf_op jit(solution)/shard_map/cond/branch_0_fun/domain_build/pallas_call | solution.py:747
  276.3 9.8 %all-to-all-start = ((bf16[32,520,128]{2,1,0:T(8,128)(2,1)}), bf16[32,520,128]{2,1,0:T(8,128)(2,1)}, u32[]{:S(2)}, u32[]{:S(2)}) async-start(bf16[32,520,128]{2,1,0:T(8,128)(2,1)} %get-tuple-element.121), calls=%async_computation | async-start | bytes 8519680 | tf_op jit(solution)/shard_map/cond/branch_0_fun/all_to_all | solution.py:921
  286.3 1.5 collective-permute-start.8
  288.0 1.5 collective-permute-start.10
  289.8 2.4 collective-permute-start.12
  292.1 33.1 %collective-permute-done.8.refs_2_ = bf16[1536,128]{1,0:T(8,128)(2,1)S(1)} collective-permute-done((bf16[1536,128]{1,0:T(8,128)(2,1)S(1)}, bf16[1536,128]{1,0:T(8,128)(2,1)S(1)}, u32[]{:S(2)}, u32[]{:S(2)}) %collective-permute-start.8) | collective-permute-done | bytes 393248 | tf_op jit(solution)/shard_map/cond/branch_0_fun/ppermute | solution.py:927
  325.5 11.5 %collective-permute-done.9.refs_3_ = bf16[1536,128]{1,0:T(8,128)(2,1)S(1)} collective-permute-done((bf16[1536,128]{1,0:T(8,128)(2,1)}, bf16[1536,128]{1,0:T(8,128)(2,1)S(1)}, u32[]{:S(2)}, u32[]{:S(2)}) %collective-permute-start.9) | collective-permute-done | bytes 393248 | tf_op jit(solution)/shard_map/cond/branch_0_fun/ppermute | solution.py:927
  337.0 21.3 %collective-permute-done.12.refs_6_ = bf16[1536,128]{1,0:T(8,128)(2,1)S(1)} collective-permute-done((bf16[1536,128]{1,0:T(8,128)(2,1)}, bf16[1536,128]{1,0:T(8,128)(2,1)S(1)}, u32[]{:S(2)}, u32[]{:S(2)}) %collective-permute-start.12) | collective-permute-done | bytes 393248 | tf_op jit(solution)/shard_map/cond/branch_0_fun/ppermute | solution.py:927
  358.3 10.6 %collective-permute-done.13.refs_7_ = bf16[1536,128]{1,0:T(8,128)(2,1)S(1)} collective-permute-done((bf16[1536,128]{1,0:T(8,128)(2,1)S(1)}, bf16[1536,128]{1,0:T(8,128)(2,1)S(1)}, u32[]{:S(2)}, u32[]{:S(2)}) %collective-permute-start.13) | collective-permute-done | bytes 393248 | tf_op jit(solution)/shard_map/cond/branch_0_fun/ppermute | solution.py:927
  369.7 3.4 relay_back.1
  373.1 4.7 %collective-permute-start.14 = (bf16[2056,128]{1,0:T(8,128)(2,1)}, bf16[2056,128]{1,0:T(8,128)(2,1)S(1)}, u32[]{:S(2)}, u32[]{:S(2)}) collective-permute-start(bf16[2056,128]{1,0:T(8,128)(2,1)} %get-tuple-element.140), channel_id=1, source_target_pairs={{0,1},{1,0},{2,3},{3,2},{4,5},{5,4},{6,7},{7,6},{8,9},{9,8},{10,11... | collective-permute-start | bytes 1579016 | tf_op jit(solution)/shard_map/cond/branch_0_fun/ppermute | solution.py:927
  377.8 1.5 collective-permute-start.16
  380.1 1.2 collective-permute-done.refs_1_
  381.4 5.2 %collective-permute-done.1.refs_2_ = bf16[512,128]{1,0:T(8,128)(2,1)S(1)} collective-permute-done((bf16[512,128]{1,0:T(8,128)(2,1)}, bf16[512,128]{1,0:T(8,128)(2,1)S(1)}, u32[]{:S(2)}, u32[]{:S(2)}) %collective-permute-start.1) | collective-permute-done | bytes 131104 | tf_op jit(solution)/shard_map/cond/branch_0_fun/ppermute | solution.py:927
  387.5 1.5 collective-permute-start.4
  389.0 5.3 %collective-permute-done.3.refs_4_ = bf16[512,128]{1,0:T(8,128)(2,1)S(1)} collective-permute-done((bf16[512,128]{1,0:T(8,128)(2,1)}, bf16[512,128]{1,0:T(8,128)(2,1)S(1)}, u32[]{:S(2)}, u32[]{:S(2)}) %collective-permute-start.3) | collective-permute-done | bytes 131104 | tf_op jit(solution)/shard_map/cond/branch_0_fun/ppermute | solution.py:927
  394.9 1.7 collective-permute-start.6
  396.7 4.9 %collective-permute-done.5.refs_6_ = bf16[512,128]{1,0:T(8,128)(2,1)S(1)} collective-permute-done((bf16[512,128]{1,0:T(8,128)(2,1)S(1)}, bf16[512,128]{1,0:T(8,128)(2,1)S(1)}, u32[]{:S(2)}, u32[]{:S(2)}) %collective-permute-start.5) | collective-permute-done | bytes 131104 | tf_op jit(solution)/shard_map/cond/branch_0_fun/ppermute | solution.py:927
  402.3 6.8 %collect_blocks.2 = (f32[64,128,128]{2,1,0:T(8,128)}, f32[1,1]{1,0:T(1,128)}) custom-call(s32[2,64]{1,0:T(2,128)S(1)} %copy-done.36, bf16[32,520,128]{2,1,0:T(8,128)(2,1)} %all-to-all-done.returned, bf16[512,128]{1,0:T(8,128)(2,1)} %get-tuple-element.122.refs_0_, bf16[512,128]{1,0:T(8,128)(2,1)} %copy-done.26, bf16[512,128]{1,0:T(8,128)(2,1)} %copy-done.27, ...), custom_call_target="tpu_custom_call" | custom-call | flops 1000 | bytes 8388608 | tf_op jit(solution)/shard_map/cond/branch_0_fun/collect_blocks/pallas_call | solution.py:832
  409.1 6.2 %collective-permute-done.15.refs_1_ = bf16[2056,128]{1,0:T(8,128)(2,1)S(1)} collective-permute-done((bf16[2056,128]{1,0:T(8,128)(2,1)}, bf16[2056,128]{1,0:T(8,128)(2,1)S(1)}, u32[]{:S(2)}, u32[]{:S(2)}) %collective-permute-start.15) | collective-permute-done | bytes 526368 | tf_op jit(solution)/shard_map/cond/branch_0_fun/ppermute | solution.py:927
  415.3 13.2 %collective-permute-done.16.refs_2_ = bf16[2056,128]{1,0:T(8,128)(2,1)S(1)} collective-permute-done((bf16[2056,128]{1,0:T(8,128)(2,1)}, bf16[2056,128]{1,0:T(8,128)(2,1)S(1)}, u32[]{:S(2)}, u32[]{:S(2)}) %collective-permute-start.16) | collective-permute-done | bytes 526368 | tf_op jit(solution)/shard_map/cond/branch_0_fun/ppermute | solution.py:927
  429.2 5.7 %add_blocks.1 = f32[64,128,128]{2,1,0:T(8,128)} custom-call(s32[2,64]{1,0:T(2,128)S(1)} %copy-done.36, f32[64,128,128]{2,1,0:T(8,128)} %get-tuple-element.130.partial, bf16[2056,128]{1,0:T(8,128)(2,1)} %copy-done.15, bf16[2056,128]{1,0:T(8,128)(2,1)} %copy-done.16, bf16[2056,128]{1,0:T(8,128)(2,1)} %copy-done.17), custom_call_target="tpu_custom_call", output_to_operand_aliasing={{}: (1, {})} | custom-call | tf_op jit(solution)/shard_map/cond/branch_0_fun/add_blocks/pallas_call | solution.py:901
  435.2 0.9 copy-done.1
  (131 shorter events, 7.2 us)
Async XLA Ops:
  0.6 208.3 %copy-start = (f32[10,2048]{1,0:T(8,128)S(1)}, f32[10,2048]{1,0:T(8,128)}, u32[]{:S(2)}) copy-start(f32[10,2048]{1,0:T(8,128)} %param.16) | copy-start | bytes 245764
  15.7 168.7 %copy-start.46 = (bf16[520,128]{1,0:T(8,128)(2,1)S(1)}, bf16[520,128]{1,0:T(8,128)(2,1)}, u32[]{:S(2)}) copy-start(bf16[520,128]{1,0:T(8,128)(2,1)} %get-tuple-element.196) | copy-start | bytes 399364
  15.7 170.5 %copy-start.45 = (bf16[520,128]{1,0:T(8,128)(2,1)S(1)}, bf16[520,128]{1,0:T(8,128)(2,1)}, u32[]{:S(2)}) copy-start(bf16[520,128]{1,0:T(8,128)(2,1)} %get-tuple-element.197) | copy-start | bytes 399364
  15.7 172.0 %copy-start.44 = (bf16[520,128]{1,0:T(8,128)(2,1)S(1)}, bf16[520,128]{1,0:T(8,128)(2,1)}, u32[]{:S(2)}) copy-start(bf16[520,128]{1,0:T(8,128)(2,1)} %get-tuple-element.198) | copy-start | bytes 399364
  15.7 184.2 %copy-start.3 = (f32[128,128]{1,0:T(8,128)S(1)}, f32[128,128]{1,0:T(8,128)}, u32[]{:S(2)}) copy-start(f32[128,128]{1,0:T(8,128)} %param.19) | copy-start | bytes 196612
  15.7 184.3 %copy-start.4 = (f32[128,128]{1,0:T(8,128)S(1)}, f32[128,128]{1,0:T(8,128)}, u32[]{:S(2)}) copy-start(f32[128,128]{1,0:T(8,128)} %param.20) | copy-start | bytes 196612
  15.7 221.4 %all-to-all-start.4 = ((bf16[32,512,128]{2,1,0:T(8,128)(2,1)}), bf16[32,512,128]{2,1,0:T(8,128)(2,1)}, u32[]{:S(2)}, u32[]{:S(2)}) async-start(bf16[32,512,128]{2,1,0:T(8,128)(2,1)} %direct_blocks.3), calls=%async_computation.4 | async-start | bytes 8388608 | tf_op jit(solution)/shard_map/all_to_all | solution.py:921
  21.9 81.4 %collective-permute-start.24 = (bf16[2056,128]{1,0:T(8,128)(2,1)}, bf16[2056,128]{1,0:T(8,128)(2,1)S(1)}, u32[]{:S(2)}, u32[]{:S(2)}) collective-permute-start(bf16[2056,128]{1,0:T(8,128)(2,1)} %get-tuple-element.199), channel_id=1, source_target_pairs={{0,1},{1,0},{2,3},{3,2},{4,5},{5,4},{6,7},{7,6},{8,9},{9,8},{10,11... | collective-permute-start | bytes 1579016 | tf_op jit(solution)/shard_map/ppermute | solution.py:927
  22.3 125.6 %collective-permute-start.25 = (bf16[2056,128]{1,0:T(8,128)(2,1)S(1)}, bf16[2056,128]{1,0:T(8,128)(2,1)S(1)}, u32[]{:S(2)}, u32[]{:S(2)}) collective-permute-start(bf16[2056,128]{1,0:T(8,128)(2,1)S(1)} %copy-done.40), channel_id=1, source_target_pairs={{0,2},{1,3},{2,0},{3,1},{4,6},{5,7},{6,4},{7,5},{8,10},{9,11},{10,... | collective-permute-start | bytes 1579016 | tf_op jit(solution)/shard_map/ppermute | solution.py:927
  24.9 136.6 %collective-permute-start.26 = (bf16[2056,128]{1,0:T(8,128)(2,1)S(1)}, bf16[2056,128]{1,0:T(8,128)(2,1)S(1)}, u32[]{:S(2)}, u32[]{:S(2)}) collective-permute-start(bf16[2056,128]{1,0:T(8,128)(2,1)S(1)} %copy-done.39), channel_id=1, source_target_pairs={{0,3},{1,2},{2,1},{3,0},{4,7},{5,6},{6,5},{7,4},{8,11},{9,10},{10,... | collective-permute-start | bytes 1579016 | tf_op jit(solution)/shard_map/ppermute | solution.py:927
  25.4 145.9 %collective-permute-start.17 = (bf16[520,128]{1,0:T(8,128)(2,1)}, bf16[520,128]{1,0:T(8,128)(2,1)S(1)}, u32[]{:S(2)}, u32[]{:S(2)}) collective-permute-start(bf16[520,128]{1,0:T(8,128)(2,1)} %get-tuple-element.192), channel_id=1, source_target_pairs={{0,4},{4,0},{8,12},{12,8},{16,20},{20,16},{24,28},{28,24},{1,5},{5... | collective-permute-start | bytes 399368 | tf_op jit(solution)/shard_map/ppermute | solution.py:927
  103.3 58.2 %copy-start.12 = (bf16[2056,128]{1,0:T(8,128)(2,1)}, bf16[2056,128]{1,0:T(8,128)(2,1)S(1)}, u32[]{:S(2)}) copy-start(bf16[2056,128]{1,0:T(8,128)(2,1)S(1)} %collective-permute-done.24.refs_0_) | copy-start | bytes 1579012
  169.2 27.8 %collective-permute-start.27 = (bf16[1544,128]{1,0:T(8,128)(2,1)}, bf16[1544,128]{1,0:T(8,128)(2,1)}, u32[]{:S(2)}, u32[]{:S(2)}) collective-permute-start(bf16[1544,128]{1,0:T(8,128)(2,1)} %get-tuple-element.203), channel_id=1, source_target_pairs={{0,4},{4,0},{8,12},{12,8},{16,20},{20,16},{24,28},{28,24},{1,5},{5... | collective-permute-start | bytes 1185800 | tf_op jit(solution)/shard_map/ppermute | solution.py:927
  169.3 29.5 %collective-permute-start.28 = (bf16[1544,128]{1,0:T(8,128)(2,1)}, bf16[1544,128]{1,0:T(8,128)(2,1)}, u32[]{:S(2)}, u32[]{:S(2)}) collective-permute-start(bf16[1544,128]{1,0:T(8,128)(2,1)} %get-tuple-element.204), channel_id=1, source_target_pairs={{0,8},{4,12},{8,0},{12,4},{16,24},{20,28},{24,16},{28,20},{1,9},{5... | collective-permute-start | bytes 1185800 | tf_op jit(solution)/shard_map/ppermute | solution.py:927
  169.3 15.1 %collective-permute-start.18 = (bf16[520,128]{1,0:T(8,128)(2,1)}, bf16[520,128]{1,0:T(8,128)(2,1)S(1)}, u32[]{:S(2)}, u32[]{:S(2)}) collective-permute-start(bf16[520,128]{1,0:T(8,128)(2,1)} %get-tuple-element.193), channel_id=1, source_target_pairs={{0,8},{4,12},{8,0},{12,4},{16,24},{20,28},{24,16},{28,20},{1,9},{5... | collective-permute-start | bytes 399368 | tf_op jit(solution)/shard_map/ppermute | solution.py:927
  171.4 14.8 %collective-permute-start.19 = (bf16[520,128]{1,0:T(8,128)(2,1)}, bf16[520,128]{1,0:T(8,128)(2,1)S(1)}, u32[]{:S(2)}, u32[]{:S(2)}) collective-permute-start(bf16[520,128]{1,0:T(8,128)(2,1)} %get-tuple-element.194), channel_id=1, source_target_pairs={{0,12},{4,8},{8,4},{12,0},{16,28},{20,24},{24,20},{28,16},{1,13},{... | collective-permute-start | bytes 399368 | tf_op jit(solution)/shard_map/ppermute | solution.py:927
  171.4 16.3 %collective-permute-start.20 = (bf16[520,128]{1,0:T(8,128)(2,1)}, bf16[520,128]{1,0:T(8,128)(2,1)S(1)}, u32[]{:S(2)}, u32[]{:S(2)}) collective-permute-start(bf16[520,128]{1,0:T(8,128)(2,1)} %get-tuple-element.195), channel_id=1, source_target_pairs={{0,16},{4,20},{8,24},{12,28},{16,0},{20,4},{24,8},{28,12},{1,17},{... | collective-permute-start | bytes 399368 | tf_op jit(solution)/shard_map/ppermute | solution.py:927
  184.4 11.0 %collective-permute-start.21 = (bf16[520,128]{1,0:T(8,128)(2,1)S(1)}, bf16[520,128]{1,0:T(8,128)(2,1)S(1)}, u32[]{:S(2)}, u32[]{:S(2)}) collective-permute-start(bf16[520,128]{1,0:T(8,128)(2,1)S(1)} %copy-done.46), channel_id=1, source_target_pairs={{0,20},{4,16},{8,28},{12,24},{16,4},{20,0},{24,12},{28,8},{1,21},{... | collective-permute-start | bytes 399368 | tf_op jit(solution)/shard_map/ppermute | solution.py:927
  186.2 9.3 %collective-permute-start.22 = (bf16[520,128]{1,0:T(8,128)(2,1)S(1)}, bf16[520,128]{1,0:T(8,128)(2,1)S(1)}, u32[]{:S(2)}, u32[]{:S(2)}) collective-permute-start(bf16[520,128]{1,0:T(8,128)(2,1)S(1)} %copy-done.45), channel_id=1, source_target_pairs={{0,24},{4,28},{8,16},{12,20},{16,8},{20,12},{24,0},{28,4},{1,25},{... | collective-permute-start | bytes 399368 | tf_op jit(solution)/shard_map/ppermute | solution.py:927
  187.7 7.9 %collective-permute-start.23 = (bf16[520,128]{1,0:T(8,128)(2,1)S(1)}, bf16[520,128]{1,0:T(8,128)(2,1)S(1)}, u32[]{:S(2)}, u32[]{:S(2)}) collective-permute-start(bf16[520,128]{1,0:T(8,128)(2,1)S(1)} %copy-done.44), channel_id=1, source_target_pairs={{0,28},{4,24},{8,20},{12,16},{16,12},{20,8},{24,4},{28,0},{1,29},{... | collective-permute-start | bytes 399368 | tf_op jit(solution)/shard_map/ppermute | solution.py:927
  195.4 14.6 %collective-permute-start.29 = (bf16[1544,128]{1,0:T(8,128)(2,1)}, bf16[1544,128]{1,0:T(8,128)(2,1)}, u32[]{:S(2)}, u32[]{:S(2)}) collective-permute-start(bf16[1544,128]{1,0:T(8,128)(2,1)} %get-tuple-element.205), channel_id=1, source_target_pairs={{0,12},{4,8},{8,4},{12,0},{16,28},{20,24},{24,20},{28,16},{1,13},{... | collective-permute-start | bytes 1185800 | tf_op jit(solution)/shard_map/ppermute | solution.py:927
  195.5 29.4 %collective-permute-start.30 = (bf16[1544,128]{1,0:T(8,128)(2,1)}, bf16[1544,128]{1,0:T(8,128)(2,1)}, u32[]{:S(2)}, u32[]{:S(2)}) collective-permute-start(bf16[1544,128]{1,0:T(8,128)(2,1)} %get-tuple-element.206), channel_id=1, source_target_pairs={{0,16},{4,20},{8,24},{12,28},{16,0},{20,4},{24,8},{28,12},{1,17},{... | collective-permute-start | bytes 1185800 | tf_op jit(solution)/shard_map/ppermute | solution.py:927
  195.6 36.0 %collective-permute-start.31 = (bf16[1544,128]{1,0:T(8,128)(2,1)}, bf16[1544,128]{1,0:T(8,128)(2,1)}, u32[]{:S(2)}, u32[]{:S(2)}) collective-permute-start(bf16[1544,128]{1,0:T(8,128)(2,1)} %get-tuple-element.207), channel_id=1, source_target_pairs={{0,20},{4,16},{8,28},{12,24},{16,4},{20,0},{24,12},{28,8},{1,21},{... | collective-permute-start | bytes 1185800 | tf_op jit(solution)/shard_map/ppermute | solution.py:927
  197.0 34.6 %collective-permute-start.32 = (bf16[1544,128]{1,0:T(8,128)(2,1)}, bf16[1544,128]{1,0:T(8,128)(2,1)}, u32[]{:S(2)}, u32[]{:S(2)}) collective-permute-start(bf16[1544,128]{1,0:T(8,128)(2,1)} %get-tuple-element.208), channel_id=1, source_target_pairs={{0,24},{4,28},{8,16},{12,20},{16,8},{20,12},{24,0},{28,4},{1,25},{... | collective-permute-start | bytes 1185800 | tf_op jit(solution)/shard_map/ppermute | solution.py:927
  198.8 32.8 %collective-permute-start.33 = (bf16[1544,128]{1,0:T(8,128)(2,1)}, bf16[1544,128]{1,0:T(8,128)(2,1)}, u32[]{:S(2)}, u32[]{:S(2)}) collective-permute-start(bf16[1544,128]{1,0:T(8,128)(2,1)} %get-tuple-element.209), channel_id=1, source_target_pairs={{0,28},{4,24},{8,20},{12,16},{16,12},{20,8},{24,4},{28,0},{1,29},{... | collective-permute-start | bytes 1185800 | tf_op jit(solution)/shard_map/ppermute | solution.py:927
  276.3 93.4 %copy-start.38 = (s32[3,16]{1,0:T(4,128)S(1)}, s32[3,16]{1,0:T(4,128)}, u32[]{:S(2)}) copy-start(s32[3,16]{1,0:T(4,128)} %get-tuple-element.131.places) | copy-start | bytes 580 | tf_op jit(solution)/shard_map/cond
  276.3 118.1 %copy-start.48 = (bf16[512,128]{1,0:T(8,128)(2,1)S(1)}, bf16[512,128]{1,0:T(8,128)(2,1)}, u32[]{:S(2)}) copy-start(bf16[512,128]{1,0:T(8,128)(2,1)} %get-tuple-element.128) | copy-start | bytes 393220 | tf_op jit(solution)/shard_map/cond
  276.3 118.6 %copy-start.47 = (bf16[512,128]{1,0:T(8,128)(2,1)S(1)}, bf16[512,128]{1,0:T(8,128)(2,1)}, u32[]{:S(2)}) copy-start(bf16[512,128]{1,0:T(8,128)(2,1)} %get-tuple-element.129) | copy-start | bytes 393220 | tf_op jit(solution)/shard_map/cond
  276.3 126.0 %copy-start.36 = (s32[2,64]{1,0:T(2,128)S(1)}, s32[2,64]{1,0:T(2,128)}, u32[]{:S(2)}) copy-start(s32[2,64]{1,0:T(2,128)} %get-tuple-element.90.places) | copy-start | bytes 1540 | tf_op jit(solution)/shard_map/cond
  276.3 125.3 %all-to-all-start = ((bf16[32,520,128]{2,1,0:T(8,128)(2,1)}), bf16[32,520,128]{2,1,0:T(8,128)(2,1)}, u32[]{:S(2)}, u32[]{:S(2)}) async-start(bf16[32,520,128]{2,1,0:T(8,128)(2,1)} %get-tuple-element.121), calls=%async_computation | async-start | bytes 8519680 | tf_op jit(solution)/shard_map/cond/branch_0_fun/all_to_all | solution.py:921
  286.1 3.7 collective-permute-start.7
  286.3 39.0 %collective-permute-start.8 = (bf16[1536,128]{1,0:T(8,128)(2,1)S(1)}, bf16[1536,128]{1,0:T(8,128)(2,1)S(1)}, u32[]{:S(2)}, u32[]{:S(2)}) collective-permute-start(bf16[1536,128]{1,0:T(8,128)(2,1)S(1)} %copy-done.42), channel_id=1, source_target_pairs={{0,8},{4,12},{8,0},{12,4},{16,24},{20,28},{24,16},{28,20},{1,9},{5... | collective-permute-start | bytes 1179656 | tf_op jit(solution)/shard_map/cond/branch_0_fun/ppermute | solution.py:927
  287.7 49.2 %collective-permute-start.9 = (bf16[1536,128]{1,0:T(8,128)(2,1)}, bf16[1536,128]{1,0:T(8,128)(2,1)S(1)}, u32[]{:S(2)}, u32[]{:S(2)}) collective-permute-start(bf16[1536,128]{1,0:T(8,128)(2,1)} %get-tuple-element.135), channel_id=1, source_target_pairs={{0,12},{4,8},{8,4},{12,0},{16,28},{20,24},{24,20},{28,16},{1,13},{... | collective-permute-start | bytes 1179656 | tf_op jit(solution)/shard_map/cond/branch_0_fun/ppermute | solution.py:927
  288.0 49.0 %collective-permute-start.10 = (bf16[1536,128]{1,0:T(8,128)(2,1)}, bf16[1536,128]{1,0:T(8,128)(2,1)S(1)}, u32[]{:S(2)}, u32[]{:S(2)}) collective-permute-start(bf16[1536,128]{1,0:T(8,128)(2,1)} %get-tuple-element.136), channel_id=1, source_target_pairs={{0,16},{4,20},{8,24},{12,28},{16,0},{20,4},{24,8},{28,12},{1,17},{... | collective-permute-start | bytes 1179656 | tf_op jit(solution)/shard_map/cond/branch_0_fun/ppermute | solution.py:927
  289.5 47.5 %collective-permute-start.11 = (bf16[1536,128]{1,0:T(8,128)(2,1)}, bf16[1536,128]{1,0:T(8,128)(2,1)S(1)}, u32[]{:S(2)}, u32[]{:S(2)}) collective-permute-start(bf16[1536,128]{1,0:T(8,128)(2,1)} %get-tuple-element.137), channel_id=1, source_target_pairs={{0,20},{4,16},{8,28},{12,24},{16,4},{20,0},{24,12},{28,8},{1,21},{... | collective-permute-start | bytes 1179656 | tf_op jit(solution)/shard_map/cond/branch_0_fun/ppermute | solution.py:927
  289.8 79.2 %copy-start.18 = (bf16[1536,128]{1,0:T(8,128)(2,1)}, bf16[1536,128]{1,0:T(8,128)(2,1)S(1)}, u32[]{:S(2)}) copy-start(bf16[1536,128]{1,0:T(8,128)(2,1)S(1)} %collective-permute-done.7.refs_1_) | copy-start | bytes 1179652 | tf_op jit(solution)/shard_map/cond
  289.8 68.5 %collective-permute-start.12 = (bf16[1536,128]{1,0:T(8,128)(2,1)}, bf16[1536,128]{1,0:T(8,128)(2,1)S(1)}, u32[]{:S(2)}, u32[]{:S(2)}) collective-permute-start(bf16[1536,128]{1,0:T(8,128)(2,1)} %get-tuple-element.138), channel_id=1, source_target_pairs={{0,24},{4,28},{8,16},{12,20},{16,8},{20,12},{24,0},{28,4},{1,25},{... | collective-permute-start | bytes 1179656 | tf_op jit(solution)/shard_map/cond/branch_0_fun/ppermute | solution.py:927
  325.2 43.7 %collective-permute-start.13 = (bf16[1536,128]{1,0:T(8,128)(2,1)S(1)}, bf16[1536,128]{1,0:T(8,128)(2,1)S(1)}, u32[]{:S(2)}, u32[]{:S(2)}) collective-permute-start(bf16[1536,128]{1,0:T(8,128)(2,1)S(1)} %copy-done.41), channel_id=1, source_target_pairs={{0,28},{4,24},{8,20},{12,16},{16,12},{20,8},{24,4},{28,0},{1,29},{... | collective-permute-start | bytes 1179656 | tf_op jit(solution)/shard_map/cond/branch_0_fun/ppermute | solution.py:927
  373.1 36.0 %collective-permute-start.14 = (bf16[2056,128]{1,0:T(8,128)(2,1)}, bf16[2056,128]{1,0:T(8,128)(2,1)S(1)}, u32[]{:S(2)}, u32[]{:S(2)}) collective-permute-start(bf16[2056,128]{1,0:T(8,128)(2,1)} %get-tuple-element.140), channel_id=1, source_target_pairs={{0,1},{1,0},{2,3},{3,2},{4,5},{5,4},{6,7},{7,6},{8,9},{9,8},{10,11... | collective-permute-start | bytes 1579016 | tf_op jit(solution)/shard_map/cond/branch_0_fun/ppermute | solution.py:927
  377.8 37.4 %collective-permute-start.15 = (bf16[2056,128]{1,0:T(8,128)(2,1)}, bf16[2056,128]{1,0:T(8,128)(2,1)S(1)}, u32[]{:S(2)}, u32[]{:S(2)}) collective-permute-start(bf16[2056,128]{1,0:T(8,128)(2,1)} %get-tuple-element.141), channel_id=1, source_target_pairs={{0,2},{1,3},{2,0},{3,1},{4,6},{5,7},{6,4},{7,5},{8,10},{9,11},{10,... | collective-permute-start | bytes 1579016 | tf_op jit(solution)/shard_map/cond/branch_0_fun/ppermute | solution.py:927
  377.8 50.6 %collective-permute-start.16 = (bf16[2056,128]{1,0:T(8,128)(2,1)}, bf16[2056,128]{1,0:T(8,128)(2,1)S(1)}, u32[]{:S(2)}, u32[]{:S(2)}) collective-permute-start(bf16[2056,128]{1,0:T(8,128)(2,1)} %get-tuple-element.142), channel_id=1, source_target_pairs={{0,3},{1,2},{2,1},{3,0},{4,7},{5,6},{6,5},{7,4},{8,11},{9,10},{10,... | collective-permute-start | bytes 1579016 | tf_op jit(solution)/shard_map/cond/branch_0_fun/ppermute | solution.py:927
  379.4 1.9 collective-permute-start
  380.0 6.6 %collective-permute-start.1 = (bf16[512,128]{1,0:T(8,128)(2,1)}, bf16[512,128]{1,0:T(8,128)(2,1)S(1)}, u32[]{:S(2)}, u32[]{:S(2)}) collective-permute-start(bf16[512,128]{1,0:T(8,128)(2,1)} %get-tuple-element.124), channel_id=1, source_target_pairs={{0,8},{4,12},{8,0},{12,4},{16,24},{20,28},{24,16},{28,20},{1,9},{5... | collective-permute-start | bytes 393224 | tf_op jit(solution)/shard_map/cond/branch_0_fun/ppermute | solution.py:927
  381.2 6.3 %collective-permute-start.2 = (bf16[512,128]{1,0:T(8,128)(2,1)}, bf16[512,128]{1,0:T(8,128)(2,1)S(1)}, u32[]{:S(2)}, u32[]{:S(2)}) collective-permute-start(bf16[512,128]{1,0:T(8,128)(2,1)} %get-tuple-element.125), channel_id=1, source_target_pairs={{0,12},{4,8},{8,4},{12,0},{16,28},{20,24},{24,20},{28,16},{1,13},{... | collective-permute-start | bytes 393224 | tf_op jit(solution)/shard_map/cond/branch_0_fun/ppermute | solution.py:927
  386.6 7.7 %collective-permute-start.3 = (bf16[512,128]{1,0:T(8,128)(2,1)}, bf16[512,128]{1,0:T(8,128)(2,1)S(1)}, u32[]{:S(2)}, u32[]{:S(2)}) collective-permute-start(bf16[512,128]{1,0:T(8,128)(2,1)} %get-tuple-element.126), channel_id=1, source_target_pairs={{0,16},{4,20},{8,24},{12,28},{16,0},{20,4},{24,8},{28,12},{1,17},{... | collective-permute-start | bytes 393224 | tf_op jit(solution)/shard_map/cond/branch_0_fun/ppermute | solution.py:927
  387.5 7.4 %collective-permute-start.4 = (bf16[512,128]{1,0:T(8,128)(2,1)}, bf16[512,128]{1,0:T(8,128)(2,1)S(1)}, u32[]{:S(2)}, u32[]{:S(2)}) collective-permute-start(bf16[512,128]{1,0:T(8,128)(2,1)} %get-tuple-element.127), channel_id=1, source_target_pairs={{0,20},{4,16},{8,28},{12,24},{16,4},{20,0},{24,12},{28,8},{1,21},{... | collective-permute-start | bytes 393224 | tf_op jit(solution)/shard_map/cond/branch_0_fun/ppermute | solution.py:927
  394.3 7.2 %collective-permute-start.5 = (bf16[512,128]{1,0:T(8,128)(2,1)S(1)}, bf16[512,128]{1,0:T(8,128)(2,1)S(1)}, u32[]{:S(2)}, u32[]{:S(2)}) collective-permute-start(bf16[512,128]{1,0:T(8,128)(2,1)S(1)} %copy-done.48), channel_id=1, source_target_pairs={{0,24},{4,28},{8,16},{12,20},{16,8},{20,12},{24,0},{28,4},{1,25},{... | collective-permute-start | bytes 393224 | tf_op jit(solution)/shard_map/cond/branch_0_fun/ppermute | solution.py:927
  394.9 6.7 %collective-permute-start.6 = (bf16[512,128]{1,0:T(8,128)(2,1)S(1)}, bf16[512,128]{1,0:T(8,128)(2,1)S(1)}, u32[]{:S(2)}, u32[]{:S(2)}) collective-permute-start(bf16[512,128]{1,0:T(8,128)(2,1)S(1)} %copy-done.47), channel_id=1, source_target_pairs={{0,28},{4,24},{8,20},{12,16},{16,12},{20,8},{24,4},{28,0},{1,29},{... | collective-permute-start | bytes 393224 | tf_op jit(solution)/shard_map/cond/branch_0_fun/ppermute | solution.py:927
  (35 other events, 503.5 us)
where the time goes:
time: 437 us; the launch traced here: 436 us
  waiting for transfers between devices  291 us (67%)
  Pallas kernels  81.7 us (19%)
  starting transfers between devices  47.8 us (11%)
  local copies, waits for them, and re-layouts  12.9 us (3%)
    ppermute x34, waiting for transfers between devices, swap(): lax.ppermute(array, axis, [(i, i ^ first + k) for i in range(size)])  291 us
    pallas_call x1, Pallas kernels, domain_build(): pl.pallas_call(functools.partial(domain_kernel, len(extras)), out_shape=t...  39 us
    ppermute x34, starting transfers between devices, swap(): lax.ppermute(array, axis, [(i, i ^ first + k) for i in range(size)])  31.9 us
    all_to_all x2, starting transfers between devices, exchange(): return lax.all_to_all(array, AXES, split_axis=0, concat_axis=0, tiled=True)  15.9 us
    pallas_call x1, Pallas kernels, split_blocks(): pl.pallas_call(functools.partial(split_kernel, direct, groups), out_shape...  11 us
    unnamed x49, local copies, waits for them, and re-layouts  10.7 us
  transfers between devices with their start and end apart: 36, of which 20 were waited for; matrix products, arithmetic and copies ran while one was open for 2% of the time, Pallas kernels for 5%

commit v1 on v0

--- a/solution.py
+++ b/solution.py
@@ -68,7 +68,7 @@
             d = dest[t, p]
             rank = count[d]
             count[d] = rank + 1
-            places[t, p] = d * LINE + rank
+            places[0, t * owned + p] = d * LINE + rank
             value = code[t, p].astype(jnp.float32)
             codes[d] = jnp.where((lane == rank) & (row == 0), value, codes[d])
 
@@ -84,7 +84,7 @@
         plan_kernel,
         out_shape=(
             jax.ShapeDtypeStruct((domains, META, NBF), jnp.bfloat16),
-            jax.ShapeDtypeStruct((copies, owned), jnp.int32),
+            jax.ShapeDtypeStruct((1, copies * owned), jnp.int32),
         ),
         in_specs=[smem_spec(), smem_spec()],
         out_specs=(any_spec(), smem_spec()),
@@ -98,111 +98,130 @@
     )(dest.T, code.T)
 
 
+def spread(line):
+    return jnp.broadcast_to(line, (NBF, NBF)).T
+
+
 def split_kernel(direct, groups, dest, code, density, *refs):
     copies, owned = dest.shape
     rows_x, rows_z = groups
     domains = rows_x * rows_z
     shift = rows_z.bit_length() - 1
-    *panels, places = refs[:-7]
-    count, pool, table, blocks, ints, codes16, sems = refs[-7:]
+    *panels, lists = refs[:-6]
+    wide, stage, blocks, _, codes16, sems = refs[-6:]
     load = pltpu.make_async_copy(density, blocks, sems.at[0])
     load.start()
-    ints[...] = jnp.full(ints.shape, -1, jnp.int32)
-    fill = pltpu.make_async_copy(ints, table, sems.at[1])
-    fill.start()
-
-    @pl.loop(0, domains)
-    def _(d):
-        count[d] = 0
-
-    for k in range(rows_z + 2):
-        pool[k] = 0
-    live, over = rows_z, rows_z + 1
     me_x, me_z = lax.axis_index("gx"), lax.axis_index("gy")
-    fill.wait()
-    load.wait()
-
-    @pl.loop(0, owned)
-    def _(p):
-        for t in range(copies):
-            d = dest[t, p]
-            value = code[t, p]
-            rank = count[d]
-            count[d] = rank + 1
-            target = d >> shift
-            near = target ^ me_x
-            far = (d & (rows_z - 1)) ^ me_z
-            places[t, p] = d * LINE + rank
-
-            @pl.when((rank < direct) & (far == 0))
-            def _():
-                table[near, 1, rank] = value
-
-            @pl.when((rank < direct) & (far != 0))
-            def _():
-                table[rows_x + far - 1, 2, target * direct + rank] = value
-
-            @pl.when((rank >= direct) & (far == 0))
-            def _():
-                slot = rank - direct
-                table[near, 0, slot] = value
-                places[t, p] = (domains + near) * LINE + slot
-                pool[live] = pool[live] + 1
-                for k in range(rows_x):
-
-                    @pl.when(near == k)
-                    def _():
-                        pltpu.make_async_copy(blocks.at[p], panels[k].at[block_rows(slot)], sems.at[2]).start()
-
-            @pl.when((rank >= direct) & (far != 0))
-            def _():
-                taken = pool[far]
-                pool[far] = taken + 1
-                pool[over] = pool[over] | (taken >= POOL).astype(jnp.int32)
-                slot = jnp.minimum(taken, POOL - 1)
-                table[rows_x + far - 1, 0, slot] = value
-                table[rows_x + far - 1, 1, slot] = target
-                places[t, p] = (domains + rows_x + far - 1) * LINE + slot
-                pool[live] = pool[live] + 1
-                for k in range(1, rows_z):
-
-                    @pl.when(far == k)
-                    def _():
-                        ref = panels[rows_x + k - 1]
-                        pltpu.make_async_copy(blocks.at[p], ref.at[block_rows(slot)], sems.at[2]).start()
-
-    for k in range(len(panels)):
-        table[k, 3, 0] = pool[over]
-    back = pltpu.make_async_copy(table, ints, sems.at[1])
+    lane8, row8 = lane_row((META, NBF))
+
+    def flat(ref):
+        wide[...] = jnp.zeros(wide.shape, jnp.int32)
+        wide[0:copies, 0:owned] = ref[...]
+        rows = wide[...]
+        line = rows[0:1, :]
+        for t in range(1, copies):
+            moved = pltpu.roll(rows, t * owned, 1)
+            line = jnp.where(lane8[0:1] < t * owned, line, moved[t : t + 1, :])
+        return line
+
+    d = flat(dest)
+    value = flat(code).astype(jnp.float32)
+    lane = lax.broadcasted_iota(jnp.int32, (NBF, NBF), 1)
+    row = lax.broadcasted_iota(jnp.int32, (NBF, NBF), 0)
+    lane_f = lane.astype(jnp.float32)
+    before = row < lane
+
+    def earlier(key):
+        same = (spread(key) == key) & before
+        return jnp.sum(jnp.where(same, 1.0, 0.0), axis=0, keepdims=True)
+
+    target = lax.shift_right_logical(d, shift)
+    near = (target ^ me_x).astype(jnp.float32)
+    far_i = (d & (rows_z - 1)) ^ me_z
+    far = far_i.astype(jnp.float32)
+    target = target.astype(jnp.float32)
+    rank = earlier(d.astype(jnp.float32))
+    late = rank >= direct
+    home = far_i == 0
+    spill = jnp.where(late, jnp.where(home, 0.0, 1.0), 0.0)
+    close = jnp.where(late, jnp.where(home, 1.0, 0.0), 0.0)
+    taken = earlier(far * spill)
+    over = jnp.max(jnp.where(taken >= POOL, spill, 0.0), axis=1, keepdims=True)
+    slot = jnp.where(home, rank - direct, jnp.minimum(taken, POOL - 1.0))
+    kept = jnp.where(taken >= POOL, 0.0, spill)
+    extra = kept + close
+    entry = jnp.where(home, near, rows_x - 1.0 + far)
+    place = jnp.where(late, (domains + entry) * LINE + slot, d.astype(jnp.float32) * LINE + rank)
+    order = jnp.sum(jnp.where(before, spread(extra), 0.0), axis=0, keepdims=True)
+    pick = jnp.where(spread(order) == lane_f, spread(extra), 0.0)
+    listed = jnp.sum(pick * row.astype(jnp.float32), axis=0, keepdims=True)
+    listed_entry = jnp.sum(pick * spread(entry), axis=0, keepdims=True)
+    listed_slot = jnp.sum(pick * spread(slot), axis=0, keepdims=True)
+    number = jnp.sum(extra, axis=1, keepdims=True)
+    out = jnp.zeros((META, NBF), jnp.float32)
+    for k, line in enumerate((place, listed, listed_entry, listed_slot, number)):
+        out = jnp.where(row8 == k, jnp.broadcast_to(line, (META, NBF)), out)
+    stage[...] = out.astype(jnp.int32)
+    back = pltpu.make_async_copy(stage, lists, sems.at[1])
     back.start()
-    back.wait()
-    codes16[...] = ints[...].astype(jnp.float32).astype(jnp.bfloat16)
+    rows16 = lax.broadcasted_iota(jnp.int32, (16, NBF), 0).astype(jnp.float32)
+
+    def table(mark, amount, cell):
+        left = jnp.where(rows16 == entry, (amount + 1.0) * mark, 0.0).astype(jnp.bfloat16)
+        right = jnp.where(spread(cell) == lane_f, 1.0, 0.0).astype(jnp.bfloat16)
+        return jnp.dot(left, right, preferred_element_type=jnp.float32) - 1.0
+
+    early = jnp.where(late, 0.0, 1.0)
+    own = jnp.where(home, early, 0.0)
+    away = jnp.where(home, 0.0, early)
+    tables = (
+        table(extra, value, slot),
+        table(own + kept, jnp.where(home, value, target), jnp.where(late, slot, rank)),
+        table(away, value, target * direct + rank),
+    )
+    for e in range(len(panels)):
+        cells = jnp.where(row8 == 3, jnp.broadcast_to(over, (META, NBF)), -1.0)
+        for k, cell in enumerate(tables):
+            cells = jnp.where(row8 == k, jnp.broadcast_to(cell[e : e + 1, :], (META, NBF)), cells)
+        codes16[e] = cells.astype(jnp.bfloat16)
     metas = [
         pltpu.make_async_copy(codes16.at[k], ref.at[meta_rows(ref), :], sems.at[3 + k]) for k, ref in enumerate(panels)
     ]
     for copy in metas:
         copy.start()
-
-    @pl.loop(0, pool[live])
-    def _(k):
-        pltpu.make_async_copy(blocks.at[0], panels[0].at[block_rows(0)], sems.at[2]).wait()
+    load.wait()
+    back.wait()
+
+    @pl.loop(0, lists[4, 0])
+    def _(k):
+        p = lax.rem(lists[1, k], owned)
+        e = lists[2, k]
+        rows = block_rows(lists[3, k])
+        for j, ref in enumerate(panels):
+
+            @pl.when(e == j)
+            def _():
+                pltpu.make_async_copy(blocks.at[p], ref.at[rows], sems.at[2]).start()
 
     for copy in metas:
         copy.wait()
 
+    @pl.loop(0, lists[4, 0])
+    def _(k):
+        pltpu.make_async_copy(blocks.at[0], panels[0].at[block_rows(0)], sems.at[2]).wait()
+
 
 def split_blocks(density, dest, code, direct, groups):
-    owned, copies = dest.shape
+    owned, _ = dest.shape
     panels = [panel(direct)] * groups[0] + [panel(POOL)] * (groups[1] - 1)
     return pl.pallas_call(
         functools.partial(split_kernel, direct, groups),
-        out_shape=(*panels, jax.ShapeDtypeStruct((copies, owned), jnp.int32)),
-        in_specs=[smem_spec(), smem_spec(), any_spec()],
+        out_shape=(*panels, jax.ShapeDtypeStruct((META, NBF), jnp.int32)),
+        in_specs=[vmem_spec(), vmem_spec(), any_spec()],
         out_specs=(any_spec(),) * len(panels) + (smem_spec(),),
         scratch_shapes=[
-            pltpu.SMEM((groups[0] * groups[1],), jnp.int32),
-            pltpu.SMEM((LINE,), jnp.int32),
-            pltpu.SMEM((len(panels), META, NBF), jnp.int32),
+            pltpu.VMEM((META, NBF), jnp.int32),
+            pltpu.VMEM((META, NBF), jnp.int32),
             pltpu.VMEM((owned, NBF, NBF), jnp.bfloat16),
             pltpu.VMEM((len(panels), META, NBF), jnp.int32),
             pltpu.VMEM((len(panels), META, NBF), jnp.bfloat16),
@@ -212,8 +231,8 @@
     )(dest.T, code.T, density)
 
 
-def direct_kernel(places, density, out, blocks, live, load_sem, out_sem):
-    copies, owned = places.shape
+def direct_kernel(copies, places, density, out, blocks, live, load_sem, out_sem):
+    owned = blocks.shape[0]
     domains = out.shape[0]
     load = pltpu.make_async_copy(density, blocks, load_sem)
     load.start()
@@ -223,8 +242,8 @@
     @pl.loop(0, owned)
     def _(p):
         for t in range(copies):
-            entry = places[t, p] // LINE
-            rows = block_rows(places[t, p] - entry * LINE)
+            entry = places[0, t * owned + p] // LINE
+            rows = block_rows(places[0, t * owned + p] - entry * LINE)
 
             @pl.when(entry < domains)
             def _():
@@ -236,9 +255,9 @@
         pltpu.make_async_copy(blocks.at[0], out.at[0, block_rows(0)], out_sem).wait()
 
 
-def direct_blocks(places, density, domains, direct):
+def direct_blocks(places, density, domains, direct, copies):
     return pl.pallas_call(
-        direct_kernel,
+        functools.partial(direct_kernel, copies),
         out_shape=jax.ShapeDtypeStruct((domains, direct * NBF, NBF), jnp.bfloat16),
         in_specs=[smem_spec(), any_spec()],
         out_specs=any_spec(),
@@ -774,9 +793,9 @@
 
 
 def collect_kernel(scale, places, returned, *refs):
-    extras = refs[:-8]
-    fock, energy, parts, result, meta, in_sem, out_sem, meta_sem = refs[-8:]
-    copies, owned = places.shape
+    extras = refs[:-9]
+    fock, energy, listed, parts, result, meta, in_sem, out_sem, meta_sem = refs[-9:]
+    owned, copies = parts.shape[:2]
     sources = returned.shape[0]
     meta_in = pltpu.make_async_copy(returned.at[:, meta_rows(returned), :], meta, meta_sem)
     meta_in.start()
@@ -784,8 +803,8 @@
     @pl.loop(0, owned)
     def _(p):
         for t in range(copies):
-            entry = places[t, p] // LINE
-            rows = block_rows(places[t, p] - entry * LINE)
+            entry = places[0, t * owned + p] // LINE
+            rows = block_rows(places[0, t * owned + p] - entry * LINE)
 
             @pl.when(entry < sources)
             def _():
@@ -808,12 +827,21 @@
     per_source = jnp.sum(jnp.sum(sent, axis=0), axis=0, keepdims=True)
     energy[...] = jnp.sum(per_source, axis=1, keepdims=True) * scale
     last = (sources + len(extras)) * LINE
+    listed[owned] = 0
 
     @pl.loop(0, owned)
     def _(p):
+        hits = [places[0, t * owned + p] >= last for t in range(copies)]
+
+        @pl.when(functools.reduce(jnp.logical_or, hits))
+        def _():
+            k = listed[owned]
+            listed[k] = p
+            listed[owned] = k + 1
+
         total = jnp.zeros((NBF, NBF), jnp.float32)
         for t in range(copies):
-            here = places[t, p] < last
+            here = places[0, t * owned + p] < last
 
             @pl.when(here)
             def _():
@@ -826,17 +854,17 @@
     pltpu.make_async_copy(result, fock, out_sem).wait()
 
 
-def collect_blocks(places, returned, extras, scale):
-    copies, owned = places.shape
+def collect_blocks(places, returned, extras, scale, owned, copies):
     sources = returned.shape[0]
     return pl.pallas_call(
         functools.partial(collect_kernel, scale),
         out_shape=(
             jax.ShapeDtypeStruct((owned, NBF, NBF), jnp.float32),
             jax.ShapeDtypeStruct((1, 1), jnp.float32),
+            jax.ShapeDtypeStruct((owned + 1,), jnp.int32),
         ),
         in_specs=[smem_spec()] + [any_spec()] * (1 + len(extras)),
-        out_specs=(any_spec(), vmem_spec()),
+        out_specs=(any_spec(), vmem_spec(), smem_spec()),
         scratch_shapes=[
             pltpu.VMEM((owned, copies, NBF, NBF), jnp.bfloat16),
             pltpu.VMEM((owned, NBF, NBF), jnp.float32),
@@ -850,38 +878,32 @@
     )(places, returned, *extras)
 
 
-def add_kernel(first, places, partial, *refs):
-    extras = refs[:-8]
-    fock, parts, result, listed, live, in_sem, fock_sem, out_sem = refs[-8:]
-    copies, owned = places.shape
-    live[0] = 0
-
-    @pl.loop(0, owned)
-    def _(p):
-        hits = [places[t, p] >= first * LINE for t in range(copies)]
-
-        @pl.when(functools.reduce(jnp.logical_or, hits))
-        def _():
-            k = live[0]
-            listed[k] = p
-            live[0] = k + 1
-            pltpu.make_async_copy(partial.at[p], result.at[k], fock_sem.at[k]).start()
-            for t in range(copies):
-                entry = places[t, p] // LINE
-                rows = block_rows(places[t, p] - entry * LINE)
-                for e, ref in enumerate(extras):
-
-                    @pl.when(entry == first + e)
-                    def _():
-                        pltpu.make_async_copy(ref.at[rows], parts.at[k, t], in_sem.at[k]).start()
-
-    @pl.loop(0, live[0])
+def add_kernel(first, places, listed, partial, *refs):
+    extras = refs[:-6]
+    fock, parts, result, in_sem, fock_sem, out_sem = refs[-6:]
+    owned, copies = parts.shape[:2]
+    number = listed[owned]
+
+    @pl.loop(0, number)
+    def _(k):
+        p = listed[k]
+        pltpu.make_async_copy(partial.at[p], result.at[k], fock_sem.at[k]).start()
+        for t in range(copies):
+            entry = places[0, t * owned + p] // LINE
+            rows = block_rows(places[0, t * owned + p] - entry * LINE)
+            for e, ref in enumerate(extras):
+
+                @pl.when(entry == first + e)
+                def _():
+                    pltpu.make_async_copy(ref.at[rows], parts.at[k, t], in_sem.at[k]).start()
+
+    @pl.loop(0, number)
     def _(k):
         p = listed[k]
         pltpu.make_async_copy(partial.at[p], result.at[k], fock_sem.at[k]).wait()
         total = result[k]
         for t in range(copies):
-            here = places[t, p] >= first * LINE
+            here = places[0, t * owned + p] >= first * LINE
 
             @pl.when(here)
             def _():
@@ -891,30 +913,28 @@
         result[k] = total
         pltpu.make_async_copy(result.at[k], fock.at[p], out_sem).start()
 
-    @pl.loop(0, live[0])
+    @pl.loop(0, number)
     def _(k):
         pltpu.make_async_copy(result.at[0], fock.at[0], out_sem).wait()
 
 
-def add_blocks(places, partial, extras, first):
-    copies, owned = places.shape
+def add_blocks(places, listed, partial, extras, first, copies):
+    owned = partial.shape[0]
     return pl.pallas_call(
         functools.partial(add_kernel, first),
         out_shape=jax.ShapeDtypeStruct(partial.shape, partial.dtype),
-        in_specs=[smem_spec()] + [any_spec()] * (1 + len(extras)),
+        in_specs=[smem_spec()] * 2 + [any_spec()] * (1 + len(extras)),
         out_specs=any_spec(),
-        input_output_aliases={1: 0},
+        input_output_aliases={2: 0},
         scratch_shapes=[
             pltpu.VMEM((owned, copies, NBF, NBF), jnp.bfloat16),
             pltpu.VMEM((owned, NBF, NBF), jnp.float32),
-            pltpu.SMEM((owned,), jnp.int32),
-            pltpu.SMEM((1,), jnp.int32),
             pltpu.SemaphoreType.DMA((owned,)),
             pltpu.SemaphoreType.DMA((owned,)),
             pltpu.SemaphoreType.DMA,
         ],
         name="add_blocks",
-    )(places, partial, *extras)
+    )(places, listed, partial, *extras)
 
 
 def exchange(array):
@@ -946,12 +966,12 @@
     def plain():
         heads, places = plan_blocks(dest, code, domains)
         lists = scan(exchange(heads), [], capacity)
-        inbound = exchange(direct_blocks(places, density, domains, capacity))
+        inbound = exchange(direct_blocks(places, density, domains, capacity, copies))
         (replies,) = domain_build(lists, inbound, [], *fixed)
-        fock, energy = collect_blocks(places, exchange(replies), [], scale)
+        fock, energy, _ = collect_blocks(places, exchange(replies), [], scale, owned, copies)
         return fock, energy[0, 0]
 
-    if capacity < 8:
+    if capacity < 8 or copies * owned != NBF:
         return plain()
     direct = capacity // 2
     ranks = (rows_z - 1) * (capacity - direct)
@@ -959,7 +979,7 @@
     *panels, places = split_blocks(density, dest, code, direct, groups)
     lines_in = swap(panels[rows_x:], "gy", 1)
     near_in = swap(panels[:rows_x], "gx", 0)
-    outgoing = direct_blocks(places, density, domains, direct)
+    outgoing = direct_blocks(places, density, domains, direct, copies)
     inbound = exchange(outgoing)
     *relayed, relay_places = relay(lines_in, rows_x, ranks, direct)
     relayed_in = swap(relayed, "gx", 0)
@@ -971,8 +991,8 @@
         near_back = swap(others[:rows_x], "gx", 0)
         returned = exchange(replies)
         lines_back = swap(relay_back(relay_places, relayed_back), "gy", 1)
-        fock, energy = collect_blocks(places, returned, near_back, scale)
-        return add_blocks(places, fock, lines_back, domains + rows_x), energy[0, 0]
+        fock, energy, listed = collect_blocks(places, returned, near_back, scale, owned, copies)
+        return add_blocks(places, listed, fock, lines_back, domains + rows_x, copies), energy[0, 0]
 
     return lax.cond(raised[0] > 0, plain, split)
 

time: 437 us -> 429 us (0.982)
  Pallas kernels: 81.7 us -> 73.9 us
    pallas_call x1, Pallas kernels: 11 us -> 4.33 us  [split_blocks(): pl.pallas_call(functools.partial(split_kernel, direct, groups), out_shape...]
    unnamed x49 -> x47, local copies, waits for them, and re-layouts: 10.7 us -> 10.6 us
where the time goes in v1:
time: 429 us; the launch traced here: 428 us
  waiting for transfers between devices  291 us (68%)
  Pallas kernels  73.9 us (17%)
  starting transfers between devices  47.8 us (11%)
  local copies, waits for them, and re-layouts  12.8 us (3%)
    ppermute x34, waiting for transfers between devices, swap(): lax.ppermute(array, axis, [(i, i ^ first + k) for i in range(size)])  291 us
    pallas_call x1, Pallas kernels, domain_build(): pl.pallas_call(functools.partial(domain_kernel, len(extras)), out_shape=t...  39.1 us
    ppermute x34, starting transfers between devices, swap(): lax.ppermute(array, axis, [(i, i ^ first + k) for i in range(size)])  31.9 us
    all_to_all x2, starting transfers between devices, exchange(): return lax.all_to_all(array, AXES, split_axis=0, concat_axis=0, tiled=True)  16 us
    unnamed x47, local copies, waits for them, and re-layouts  10.6 us
  transfers between devices with their start and end apart: 36, of which 20 were waited for; matrix products, arithmetic and copies ran while one was open for 2% of the time, Pallas kernels for 5%

profile of v1, /device:TPU:8, one launch (start us, length us, event | category | flops | bytes accessed | tf_op | source)
XLA Modules:
  0.0 428.2 jit_solution(1661924089250146757)
XLA Ops:
  0.6 4.3 %split_blocks.1 = (bf16[520,128]{1,0:T(8,128)(2,1)}, bf16[520,128]{1,0:T(8,128)(2,1)}, bf16[520,128]{1,0:T(8,128)(2,1)}, bf16[520,128]{1,0:T(8,128)(2,1)}, bf16[...) custom-call(s32[2,64]{1,0:T(2,128)} %bitcast.21, ...), custom_call_target="tpu_custom_call" | custom-call | tf_op jit(solution)/shard_map/split_blocks/pallas_call | solution.py:217
  5.0 4.0 direct_blocks.3
  9.1 6.2 %all-to-all-start.4 = ((bf16[32,512,128]{2,1,0:T(8,128)(2,1)}), bf16[32,512,128]{2,1,0:T(8,128)(2,1)}, u32[]{:S(2)}, u32[]{:S(2)}) async-start(bf16[32,512,128]{2,1,0:T(8,128)(2,1)} %direct_blocks.3), calls=%async_computation.4 | async-start | bytes 8388608 | tf_op jit(solution)/shard_map/all_to_all | solution.py:941
  15.7 2.6 collective-permute-start.25
  18.9 77.9 %collective-permute-done.24.refs_0_ = bf16[2056,128]{1,0:T(8,128)(2,1)S(1)} collective-permute-done((bf16[2056,128]{1,0:T(8,128)(2,1)}, bf16[2056,128]{1,0:T(8,128)(2,1)S(1)}, u32[]{:S(2)}, u32[]{:S(2)}) %collective-permute-start.24) | collective-permute-done | bytes 526368 | tf_op jit(solution)/shard_map/ppermute | solution.py:947
  96.7 44.6 %collective-permute-done.25.refs_1_ = bf16[2056,128]{1,0:T(8,128)(2,1)S(1)} collective-permute-done((bf16[2056,128]{1,0:T(8,128)(2,1)S(1)}, bf16[2056,128]{1,0:T(8,128)(2,1)S(1)}, u32[]{:S(2)}, u32[]{:S(2)}) %collective-permute-start.25) | collective-permute-done | bytes 526368 | tf_op jit(solution)/shard_map/ppermute | solution.py:947
  141.4 13.5 %collective-permute-done.26.refs_2_ = bf16[2056,128]{1,0:T(8,128)(2,1)S(1)} collective-permute-done((bf16[2056,128]{1,0:T(8,128)(2,1)S(1)}, bf16[2056,128]{1,0:T(8,128)(2,1)S(1)}, u32[]{:S(2)}, u32[]{:S(2)}) %collective-permute-start.26) | collective-permute-done | bytes 526368 | tf_op jit(solution)/shard_map/ppermute | solution.py:947
  154.9 0.8 copy-done.17
  155.7 6.9 %relay.1 = (bf16[1544,128]{1,0:T(8,128)(2,1)}, bf16[1544,128]{1,0:T(8,128)(2,1)}, bf16[1544,128]{1,0:T(8,128)(2,1)}, bf16[1544,128]{1,0:T(8,128)(2,1)}, bf16[154...) custom-call(bf16[2056,128]{1,0:T(8,128)(2,1)} %copy-done.15, ...), custom_call_target="tpu_custom_call" | custom-call | flops 1000 | bytes 4194304 | tf_op jit(solution)/shard_map/relay/pallas_call | solution.py:511
  162.8 2.0 collective-permute-start.18
  164.8 1.6 collective-permute-start.20
  166.4 11.5 %collective-permute-done.18.refs_2_ = bf16[520,128]{1,0:T(8,128)(2,1)S(1)} collective-permute-done((bf16[520,128]{1,0:T(8,128)(2,1)}, bf16[520,128]{1,0:T(8,128)(2,1)S(1)}, u32[]{:S(2)}, u32[]{:S(2)}) %collective-permute-start.18) | collective-permute-done | bytes 133152 | tf_op jit(solution)/shard_map/ppermute | solution.py:947
  178.0 1.6 collective-permute-done.19.refs_3_
  179.7 1.5 collective-permute-start.22
  181.1 1.2 collective-permute-start.23
  182.3 6.6 %collective-permute-done.21.refs_5_ = bf16[520,128]{1,0:T(8,128)(2,1)S(1)} collective-permute-done((bf16[520,128]{1,0:T(8,128)(2,1)S(1)}, bf16[520,128]{1,0:T(8,128)(2,1)S(1)}, u32[]{:S(2)}, u32[]{:S(2)}) %collective-permute-start.21) | collective-permute-done | bytes 133152 | tf_op jit(solution)/shard_map/ppermute | solution.py:947
  189.0 1.4 collective-permute-start.31
  190.5 1.7 collective-permute-start.32
  192.2 1.2 collective-permute-start.33
  193.7 8.6 %copy.17 = bf16[2048,1536]{0,1:T(8,128)(2,1)} copy(bf16[2048,1536]{1,0:T(8,128)(2,1)} %param.15) | data formatting | bytes 12582912 | tf_op args[3]
  202.3 1.0 fusion
  203.3 14.9 %collective-permute-done.30.refs_12_ = bf16[1544,128]{1,0:T(8,128)(2,1)} collective-permute-done((bf16[1544,128]{1,0:T(8,128)(2,1)}, bf16[1544,128]{1,0:T(8,128)(2,1)}, u32[]{:S(2)}, u32[]{:S(2)}) %collective-permute-start.30) | collective-permute-done | bytes 395296 | tf_op jit(solution)/shard_map/ppermute | solution.py:947
  218.3 6.8 %collective-permute-done.31.refs_13_ = bf16[1544,128]{1,0:T(8,128)(2,1)} collective-permute-done((bf16[1544,128]{1,0:T(8,128)(2,1)}, bf16[1544,128]{1,0:T(8,128)(2,1)}, u32[]{:S(2)}, u32[]{:S(2)}) %collective-permute-start.31) | collective-permute-done | bytes 395296 | tf_op jit(solution)/shard_map/ppermute | solution.py:947
  225.0 4.9 %merge.1 = (s32[18]{0:T(128)S(1)}, s32[256]{0:T(256)S(1)}, s32[256]{0:T(256)S(1)}, s32[1]{0:T(128)}) custom-call(bf16[520,128]{1,0:T(8,128)(2,1)} %get-tuple-element.192.refs_0_, bf16[520,128]{1,0:T(8,128)(2,1)} %copy-done.5, bf16[520,128]{1,0:T(8,128)(2,1)} %copy-done.6, bf16[520,128]{1,0:T(8,128)(2,1)} %copy-done.7, bf16[520,128]{1,0:T(8,128)(2,1)} %copy-done.8, ...), custom_call_target="tpu_custom_call" | custom-call | flops 1000 | bytes 8388608 | tf_op jit(solution)/shard_map/merge/pallas_call | solution.py:394
  230.7 196.6 %conditional.1 = (f32[64,128,128]{2,1,0:T(8,128)}, f32[]{:T(128)}) conditional(s32[]{:T(128)} %bitcast.6, (s32[18]{0:T(128)S(1)}, s32[256]{0:T(256)S(1)}, s32[256]{0:T(256)S(1)}, bf16[32,512,128]{2,1,0:T(8,128)(2,1)}, bf16[520,128]{1,0:T(8,128)(2,1)}, /*index=5*/bf16[520,128]{1,0:T(8,128)(2,1)}, bf16[520,128]{1,0:T(8,128)(2,1)}, ...), branch_computations={%region_0.0_spmd, %region_1.0_spmd} | conditional | flops 3000 | bytes 73123928 | solution.py:997
  230.7 39.1 %domain_build.2 = (bf16[32,520,128]{2,1,0:T(8,128)(2,1)}, bf16[512,128]{1,0:T(8,128)(2,1)}, bf16[512,128]{1,0:T(8,128)(2,1)}, bf16[512,128]{1,0:T(8,128)(2,1)}, ...) custom-call(s32[18]{0:T(128)S(1)} %get-tuple-element.91.starts, ...), custom_call_target="tpu_custom_call" | custom-call | tf_op jit(solution)/shard_map/cond/branch_0_fun/domain_build/pallas_call | solution.py:766
  269.8 9.8 %all-to-all-start = ((bf16[32,520,128]{2,1,0:T(8,128)(2,1)}), bf16[32,520,128]{2,1,0:T(8,128)(2,1)}, u32[]{:S(2)}, u32[]{:S(2)}) async-start(bf16[32,520,128]{2,1,0:T(8,128)(2,1)} %get-tuple-element.121), calls=%async_computation | async-start | bytes 8519680 | tf_op jit(solution)/shard_map/cond/branch_0_fun/all_to_all | solution.py:941
  279.8 1.5 collective-permute-start.8
  281.5 1.5 collective-permute-start.10
  283.3 2.4 collective-permute-start.12
  285.6 33.1 %collective-permute-done.8.refs_2_ = bf16[1536,128]{1,0:T(8,128)(2,1)S(1)} collective-permute-done((bf16[1536,128]{1,0:T(8,128)(2,1)S(1)}, bf16[1536,128]{1,0:T(8,128)(2,1)S(1)}, u32[]{:S(2)}, u32[]{:S(2)}) %collective-permute-start.8) | collective-permute-done | bytes 393248 | tf_op jit(solution)/shard_map/cond/branch_0_fun/ppermute | solution.py:947
  319.0 11.5 %collective-permute-done.9.refs_3_ = bf16[1536,128]{1,0:T(8,128)(2,1)S(1)} collective-permute-done((bf16[1536,128]{1,0:T(8,128)(2,1)}, bf16[1536,128]{1,0:T(8,128)(2,1)S(1)}, u32[]{:S(2)}, u32[]{:S(2)}) %collective-permute-start.9) | collective-permute-done | bytes 393248 | tf_op jit(solution)/shard_map/cond/branch_0_fun/ppermute | solution.py:947
  330.5 21.3 %collective-permute-done.12.refs_6_ = bf16[1536,128]{1,0:T(8,128)(2,1)S(1)} collective-permute-done((bf16[1536,128]{1,0:T(8,128)(2,1)}, bf16[1536,128]{1,0:T(8,128)(2,1)S(1)}, u32[]{:S(2)}, u32[]{:S(2)}) %collective-permute-start.12) | collective-permute-done | bytes 393248 | tf_op jit(solution)/shard_map/cond/branch_0_fun/ppermute | solution.py:947
  351.8 10.6 %collective-permute-done.13.refs_7_ = bf16[1536,128]{1,0:T(8,128)(2,1)S(1)} collective-permute-done((bf16[1536,128]{1,0:T(8,128)(2,1)S(1)}, bf16[1536,128]{1,0:T(8,128)(2,1)S(1)}, u32[]{:S(2)}, u32[]{:S(2)}) %collective-permute-start.13) | collective-permute-done | bytes 393248 | tf_op jit(solution)/shard_map/cond/branch_0_fun/ppermute | solution.py:947
  363.2 3.4 relay_back.1
  366.6 4.7 %collective-permute-start.14 = (bf16[2056,128]{1,0:T(8,128)(2,1)}, bf16[2056,128]{1,0:T(8,128)(2,1)S(1)}, u32[]{:S(2)}, u32[]{:S(2)}) collective-permute-start(bf16[2056,128]{1,0:T(8,128)(2,1)} %get-tuple-element.141), channel_id=1, source_target_pairs={{0,1},{1,0},{2,3},{3,2},{4,5},{5,4},{6,7},{7,6},{8,9},{9,8},{10,11... | collective-permute-start | bytes 1579016 | tf_op jit(solution)/shard_map/cond/branch_0_fun/ppermute | solution.py:947
  371.4 1.5 collective-permute-start.16
  373.6 1.2 collective-permute-done.refs_1_
  374.9 5.2 %collective-permute-done.1.refs_2_ = bf16[512,128]{1,0:T(8,128)(2,1)S(1)} collective-permute-done((bf16[512,128]{1,0:T(8,128)(2,1)}, bf16[512,128]{1,0:T(8,128)(2,1)S(1)}, u32[]{:S(2)}, u32[]{:S(2)}) %collective-permute-start.1) | collective-permute-done | bytes 131104 | tf_op jit(solution)/shard_map/cond/branch_0_fun/ppermute | solution.py:947
  381.0 1.5 collective-permute-start.4
  382.5 5.3 %collective-permute-done.3.refs_4_ = bf16[512,128]{1,0:T(8,128)(2,1)S(1)} collective-permute-done((bf16[512,128]{1,0:T(8,128)(2,1)}, bf16[512,128]{1,0:T(8,128)(2,1)S(1)}, u32[]{:S(2)}, u32[]{:S(2)}) %collective-permute-start.3) | collective-permute-done | bytes 131104 | tf_op jit(solution)/shard_map/cond/branch_0_fun/ppermute | solution.py:947
  388.4 1.7 collective-permute-start.6
  390.2 4.9 %collective-permute-done.5.refs_6_ = bf16[512,128]{1,0:T(8,128)(2,1)S(1)} collective-permute-done((bf16[512,128]{1,0:T(8,128)(2,1)S(1)}, bf16[512,128]{1,0:T(8,128)(2,1)S(1)}, u32[]{:S(2)}, u32[]{:S(2)}) %collective-permute-start.5) | collective-permute-done | bytes 131104 | tf_op jit(solution)/shard_map/cond/branch_0_fun/ppermute | solution.py:947
  395.8 6.9 %collect_blocks.2 = (f32[64,128,128]{2,1,0:T(8,128)}, f32[1,1]{1,0:T(1,128)}, s32[65]{0:T(128)}) custom-call(s32[8,128]{1,0:T(8,128)S(1)} %get-tuple-element.90.places, bf16[32,520,128]{2,1,0:T(8,128)(2,1)} %all-to-all-done.returned, bf16[512,128]{1,0:T(8,128)(2,1)} %get-tuple-element.122.refs_0_, bf16[512,128]{1,0:T(8,128)(2,1)} %copy-done.26, ...), custom_call_target="tpu_custom_call" | custom-call | flops 1000 | bytes 8388608 | tf_op jit(solution)/shard_map/cond/branch_0_fun/collect_blocks/pallas_call | solution.py:859
  402.7 6.1 %collective-permute-done.15.refs_1_ = bf16[2056,128]{1,0:T(8,128)(2,1)S(1)} collective-permute-done((bf16[2056,128]{1,0:T(8,128)(2,1)}, bf16[2056,128]{1,0:T(8,128)(2,1)S(1)}, u32[]{:S(2)}, u32[]{:S(2)}) %collective-permute-start.15) | collective-permute-done | bytes 526368 | tf_op jit(solution)/shard_map/cond/branch_0_fun/ppermute | solution.py:947
  408.8 13.2 %collective-permute-done.16.refs_2_ = bf16[2056,128]{1,0:T(8,128)(2,1)S(1)} collective-permute-done((bf16[2056,128]{1,0:T(8,128)(2,1)}, bf16[2056,128]{1,0:T(8,128)(2,1)S(1)}, u32[]{:S(2)}, u32[]{:S(2)}) %collective-permute-start.16) | collective-permute-done | bytes 526368 | tf_op jit(solution)/shard_map/cond/branch_0_fun/ppermute | solution.py:947
  422.8 4.3 add_blocks.1
  427.3 0.9 copy-done.1
  (127 shorter events, 7.1 us)
Async XLA Ops:
  0.6 201.6 %copy-start = (f32[10,2048]{1,0:T(8,128)S(1)}, f32[10,2048]{1,0:T(8,128)}, u32[]{:S(2)}) copy-start(f32[10,2048]{1,0:T(8,128)} %param.16) | copy-start | bytes 245764
  9.1 168.8 %copy-start.45 = (bf16[520,128]{1,0:T(8,128)(2,1)S(1)}, bf16[520,128]{1,0:T(8,128)(2,1)}, u32[]{:S(2)}) copy-start(bf16[520,128]{1,0:T(8,128)(2,1)} %get-tuple-element.197) | copy-start | bytes 399364
  9.1 170.6 %copy-start.44 = (bf16[520,128]{1,0:T(8,128)(2,1)S(1)}, bf16[520,128]{1,0:T(8,128)(2,1)}, u32[]{:S(2)}) copy-start(bf16[520,128]{1,0:T(8,128)(2,1)} %get-tuple-element.198) | copy-start | bytes 399364
  9.1 172.1 %copy-start.43 = (bf16[520,128]{1,0:T(8,128)(2,1)S(1)}, bf16[520,128]{1,0:T(8,128)(2,1)}, u32[]{:S(2)}) copy-start(bf16[520,128]{1,0:T(8,128)(2,1)} %get-tuple-element.199) | copy-start | bytes 399364
  9.1 184.3 %copy-start.3 = (f32[128,128]{1,0:T(8,128)S(1)}, f32[128,128]{1,0:T(8,128)}, u32[]{:S(2)}) copy-start(f32[128,128]{1,0:T(8,128)} %param.19) | copy-start | bytes 196612
  9.1 184.4 %copy-start.4 = (f32[128,128]{1,0:T(8,128)S(1)}, f32[128,128]{1,0:T(8,128)}, u32[]{:S(2)}) copy-start(f32[128,128]{1,0:T(8,128)} %param.20) | copy-start | bytes 196612
  9.1 221.5 %all-to-all-start.4 = ((bf16[32,512,128]{2,1,0:T(8,128)(2,1)}), bf16[32,512,128]{2,1,0:T(8,128)(2,1)}, u32[]{:S(2)}, u32[]{:S(2)}) async-start(bf16[32,512,128]{2,1,0:T(8,128)(2,1)} %direct_blocks.3), calls=%async_computation.4 | async-start | bytes 8388608 | tf_op jit(solution)/shard_map/all_to_all | solution.py:941
  15.3 81.4 %collective-permute-start.24 = (bf16[2056,128]{1,0:T(8,128)(2,1)}, bf16[2056,128]{1,0:T(8,128)(2,1)S(1)}, u32[]{:S(2)}, u32[]{:S(2)}) collective-permute-start(bf16[2056,128]{1,0:T(8,128)(2,1)} %get-tuple-element.200), channel_id=1, source_target_pairs={{0,1},{1,0},{2,3},{3,2},{4,5},{5,4},{6,7},{7,6},{8,9},{9,8},{10,11... | collective-permute-start | bytes 1579016 | tf_op jit(solution)/shard_map/ppermute | solution.py:947
  15.7 125.6 %collective-permute-start.25 = (bf16[2056,128]{1,0:T(8,128)(2,1)S(1)}, bf16[2056,128]{1,0:T(8,128)(2,1)S(1)}, u32[]{:S(2)}, u32[]{:S(2)}) collective-permute-start(bf16[2056,128]{1,0:T(8,128)(2,1)S(1)} %copy-done.39), channel_id=1, source_target_pairs={{0,2},{1,3},{2,0},{3,1},{4,6},{5,7},{6,4},{7,5},{8,10},{9,11},{10,... | collective-permute-start | bytes 1579016 | tf_op jit(solution)/shard_map/ppermute | solution.py:947
  18.3 136.6 %collective-permute-start.26 = (bf16[2056,128]{1,0:T(8,128)(2,1)S(1)}, bf16[2056,128]{1,0:T(8,128)(2,1)S(1)}, u32[]{:S(2)}, u32[]{:S(2)}) collective-permute-start(bf16[2056,128]{1,0:T(8,128)(2,1)S(1)} %copy-done.38), channel_id=1, source_target_pairs={{0,3},{1,2},{2,1},{3,0},{4,7},{5,6},{6,5},{7,4},{8,11},{9,10},{10,... | collective-permute-start | bytes 1579016 | tf_op jit(solution)/shard_map/ppermute | solution.py:947
  18.9 145.9 %collective-permute-start.17 = (bf16[520,128]{1,0:T(8,128)(2,1)}, bf16[520,128]{1,0:T(8,128)(2,1)S(1)}, u32[]{:S(2)}, u32[]{:S(2)}) collective-permute-start(bf16[520,128]{1,0:T(8,128)(2,1)} %get-tuple-element.193), channel_id=1, source_target_pairs={{0,4},{4,0},{8,12},{12,8},{16,20},{20,16},{24,28},{28,24},{1,5},{5... | collective-permute-start | bytes 399368 | tf_op jit(solution)/shard_map/ppermute | solution.py:947
  96.7 58.2 %copy-start.15 = (bf16[2056,128]{1,0:T(8,128)(2,1)}, bf16[2056,128]{1,0:T(8,128)(2,1)S(1)}, u32[]{:S(2)}) copy-start(bf16[2056,128]{1,0:T(8,128)(2,1)S(1)} %collective-permute-done.24.refs_0_) | copy-start | bytes 1579012
  162.6 27.8 %collective-permute-start.27 = (bf16[1544,128]{1,0:T(8,128)(2,1)}, bf16[1544,128]{1,0:T(8,128)(2,1)}, u32[]{:S(2)}, u32[]{:S(2)}) collective-permute-start(bf16[1544,128]{1,0:T(8,128)(2,1)} %get-tuple-element.204), channel_id=1, source_target_pairs={{0,4},{4,0},{8,12},{12,8},{16,20},{20,16},{24,28},{28,24},{1,5},{5... | collective-permute-start | bytes 1185800 | tf_op jit(solution)/shard_map/ppermute | solution.py:947
  162.7 29.5 %collective-permute-start.28 = (bf16[1544,128]{1,0:T(8,128)(2,1)}, bf16[1544,128]{1,0:T(8,128)(2,1)}, u32[]{:S(2)}, u32[]{:S(2)}) collective-permute-start(bf16[1544,128]{1,0:T(8,128)(2,1)} %get-tuple-element.205), channel_id=1, source_target_pairs={{0,8},{4,12},{8,0},{12,4},{16,24},{20,28},{24,16},{28,20},{1,9},{5... | collective-permute-start | bytes 1185800 | tf_op jit(solution)/shard_map/ppermute | solution.py:947
  162.8 15.1 %collective-permute-start.18 = (bf16[520,128]{1,0:T(8,128)(2,1)}, bf16[520,128]{1,0:T(8,128)(2,1)S(1)}, u32[]{:S(2)}, u32[]{:S(2)}) collective-permute-start(bf16[520,128]{1,0:T(8,128)(2,1)} %get-tuple-element.194), channel_id=1, source_target_pairs={{0,8},{4,12},{8,0},{12,4},{16,24},{20,28},{24,16},{28,20},{1,9},{5... | collective-permute-start | bytes 399368 | tf_op jit(solution)/shard_map/ppermute | solution.py:947
  164.8 14.8 %collective-permute-start.19 = (bf16[520,128]{1,0:T(8,128)(2,1)}, bf16[520,128]{1,0:T(8,128)(2,1)S(1)}, u32[]{:S(2)}, u32[]{:S(2)}) collective-permute-start(bf16[520,128]{1,0:T(8,128)(2,1)} %get-tuple-element.195), channel_id=1, source_target_pairs={{0,12},{4,8},{8,4},{12,0},{16,28},{20,24},{24,20},{28,16},{1,13},{... | collective-permute-start | bytes 399368 | tf_op jit(solution)/shard_map/ppermute | solution.py:947
  164.8 16.3 %collective-permute-start.20 = (bf16[520,128]{1,0:T(8,128)(2,1)}, bf16[520,128]{1,0:T(8,128)(2,1)S(1)}, u32[]{:S(2)}, u32[]{:S(2)}) collective-permute-start(bf16[520,128]{1,0:T(8,128)(2,1)} %get-tuple-element.196), channel_id=1, source_target_pairs={{0,16},{4,20},{8,24},{12,28},{16,0},{20,4},{24,8},{28,12},{1,17},{... | collective-permute-start | bytes 399368 | tf_op jit(solution)/shard_map/ppermute | solution.py:947
  177.9 11.0 %collective-permute-start.21 = (bf16[520,128]{1,0:T(8,128)(2,1)S(1)}, bf16[520,128]{1,0:T(8,128)(2,1)S(1)}, u32[]{:S(2)}, u32[]{:S(2)}) collective-permute-start(bf16[520,128]{1,0:T(8,128)(2,1)S(1)} %copy-done.45), channel_id=1, source_target_pairs={{0,20},{4,16},{8,28},{12,24},{16,4},{20,0},{24,12},{28,8},{1,21},{... | collective-permute-start | bytes 399368 | tf_op jit(solution)/shard_map/ppermute | solution.py:947
  179.7 9.3 %collective-permute-start.22 = (bf16[520,128]{1,0:T(8,128)(2,1)S(1)}, bf16[520,128]{1,0:T(8,128)(2,1)S(1)}, u32[]{:S(2)}, u32[]{:S(2)}) collective-permute-start(bf16[520,128]{1,0:T(8,128)(2,1)S(1)} %copy-done.44), channel_id=1, source_target_pairs={{0,24},{4,28},{8,16},{12,20},{16,8},{20,12},{24,0},{28,4},{1,25},{... | collective-permute-start | bytes 399368 | tf_op jit(solution)/shard_map/ppermute | solution.py:947
  181.1 7.9 %collective-permute-start.23 = (bf16[520,128]{1,0:T(8,128)(2,1)S(1)}, bf16[520,128]{1,0:T(8,128)(2,1)S(1)}, u32[]{:S(2)}, u32[]{:S(2)}) collective-permute-start(bf16[520,128]{1,0:T(8,128)(2,1)S(1)} %copy-done.43), channel_id=1, source_target_pairs={{0,28},{4,24},{8,20},{12,16},{16,12},{20,8},{24,4},{28,0},{1,29},{... | collective-permute-start | bytes 399368 | tf_op jit(solution)/shard_map/ppermute | solution.py:947
  188.9 14.4 %collective-permute-start.29 = (bf16[1544,128]{1,0:T(8,128)(2,1)}, bf16[1544,128]{1,0:T(8,128)(2,1)}, u32[]{:S(2)}, u32[]{:S(2)}) collective-permute-start(bf16[1544,128]{1,0:T(8,128)(2,1)} %get-tuple-element.206), channel_id=1, source_target_pairs={{0,12},{4,8},{8,4},{12,0},{16,28},{20,24},{24,20},{28,16},{1,13},{... | collective-permute-start | bytes 1185800 | tf_op jit(solution)/shard_map/ppermute | solution.py:947
  188.9 29.4 %collective-permute-start.30 = (bf16[1544,128]{1,0:T(8,128)(2,1)}, bf16[1544,128]{1,0:T(8,128)(2,1)}, u32[]{:S(2)}, u32[]{:S(2)}) collective-permute-start(bf16[1544,128]{1,0:T(8,128)(2,1)} %get-tuple-element.207), channel_id=1, source_target_pairs={{0,16},{4,20},{8,24},{12,28},{16,0},{20,4},{24,8},{28,12},{1,17},{... | collective-permute-start | bytes 1185800 | tf_op jit(solution)/shard_map/ppermute | solution.py:947
  189.0 36.0 %collective-permute-start.31 = (bf16[1544,128]{1,0:T(8,128)(2,1)}, bf16[1544,128]{1,0:T(8,128)(2,1)}, u32[]{:S(2)}, u32[]{:S(2)}) collective-permute-start(bf16[1544,128]{1,0:T(8,128)(2,1)} %get-tuple-element.208), channel_id=1, source_target_pairs={{0,20},{4,16},{8,28},{12,24},{16,4},{20,0},{24,12},{28,8},{1,21},{... | collective-permute-start | bytes 1185800 | tf_op jit(solution)/shard_map/ppermute | solution.py:947
  190.5 34.6 %collective-permute-start.32 = (bf16[1544,128]{1,0:T(8,128)(2,1)}, bf16[1544,128]{1,0:T(8,128)(2,1)}, u32[]{:S(2)}, u32[]{:S(2)}) collective-permute-start(bf16[1544,128]{1,0:T(8,128)(2,1)} %get-tuple-element.209), channel_id=1, source_target_pairs={{0,24},{4,28},{8,16},{12,20},{16,8},{20,12},{24,0},{28,4},{1,25},{... | collective-permute-start | bytes 1185800 | tf_op jit(solution)/shard_map/ppermute | solution.py:947
  192.2 32.8 %collective-permute-start.33 = (bf16[1544,128]{1,0:T(8,128)(2,1)}, bf16[1544,128]{1,0:T(8,128)(2,1)}, u32[]{:S(2)}, u32[]{:S(2)}) collective-permute-start(bf16[1544,128]{1,0:T(8,128)(2,1)} %get-tuple-element.210), channel_id=1, source_target_pairs={{0,28},{4,24},{8,20},{12,16},{16,12},{20,8},{24,4},{28,0},{1,29},{... | collective-permute-start | bytes 1185800 | tf_op jit(solution)/shard_map/ppermute | solution.py:947
  269.8 49.0 %copy-start.40 = (bf16[1536,128]{1,0:T(8,128)(2,1)S(1)}, bf16[1536,128]{1,0:T(8,128)(2,1)}, u32[]{:S(2)}) copy-start(bf16[1536,128]{1,0:T(8,128)(2,1)} %get-tuple-element.140) | copy-start | bytes 1179652 | tf_op jit(solution)/shard_map/cond
  269.8 93.4 %copy-start.37 = (s32[3,16]{1,0:T(4,128)S(1)}, s32[3,16]{1,0:T(4,128)}, u32[]{:S(2)}) copy-start(s32[3,16]{1,0:T(4,128)} %get-tuple-element.132.places) | copy-start | bytes 580 | tf_op jit(solution)/shard_map/cond
  269.8 118.0 %copy-start.47 = (bf16[512,128]{1,0:T(8,128)(2,1)S(1)}, bf16[512,128]{1,0:T(8,128)(2,1)}, u32[]{:S(2)}) copy-start(bf16[512,128]{1,0:T(8,128)(2,1)} %get-tuple-element.128) | copy-start | bytes 393220 | tf_op jit(solution)/shard_map/cond
  269.8 118.6 %copy-start.46 = (bf16[512,128]{1,0:T(8,128)(2,1)S(1)}, bf16[512,128]{1,0:T(8,128)(2,1)}, u32[]{:S(2)}) copy-start(bf16[512,128]{1,0:T(8,128)(2,1)} %get-tuple-element.129) | copy-start | bytes 393220 | tf_op jit(solution)/shard_map/cond
  269.8 125.3 %all-to-all-start = ((bf16[32,520,128]{2,1,0:T(8,128)(2,1)}), bf16[32,520,128]{2,1,0:T(8,128)(2,1)}, u32[]{:S(2)}, u32[]{:S(2)}) async-start(bf16[32,520,128]{2,1,0:T(8,128)(2,1)} %get-tuple-element.121), calls=%async_computation | async-start | bytes 8519680 | tf_op jit(solution)/shard_map/cond/branch_0_fun/all_to_all | solution.py:941
  279.6 3.7 collective-permute-start.7
  279.8 39.0 %collective-permute-start.8 = (bf16[1536,128]{1,0:T(8,128)(2,1)S(1)}, bf16[1536,128]{1,0:T(8,128)(2,1)S(1)}, u32[]{:S(2)}, u32[]{:S(2)}) collective-permute-start(bf16[1536,128]{1,0:T(8,128)(2,1)S(1)} %copy-done.41), channel_id=1, source_target_pairs={{0,8},{4,12},{8,0},{12,4},{16,24},{20,28},{24,16},{28,20},{1,9},{5... | collective-permute-start | bytes 1179656 | tf_op jit(solution)/shard_map/cond/branch_0_fun/ppermute | solution.py:947
  281.2 49.2 %collective-permute-start.9 = (bf16[1536,128]{1,0:T(8,128)(2,1)}, bf16[1536,128]{1,0:T(8,128)(2,1)S(1)}, u32[]{:S(2)}, u32[]{:S(2)}) collective-permute-start(bf16[1536,128]{1,0:T(8,128)(2,1)} %get-tuple-element.136), channel_id=1, source_target_pairs={{0,12},{4,8},{8,4},{12,0},{16,28},{20,24},{24,20},{28,16},{1,13},{... | collective-permute-start | bytes 1179656 | tf_op jit(solution)/shard_map/cond/branch_0_fun/ppermute | solution.py:947
  281.5 49.0 %collective-permute-start.10 = (bf16[1536,128]{1,0:T(8,128)(2,1)}, bf16[1536,128]{1,0:T(8,128)(2,1)S(1)}, u32[]{:S(2)}, u32[]{:S(2)}) collective-permute-start(bf16[1536,128]{1,0:T(8,128)(2,1)} %get-tuple-element.137), channel_id=1, source_target_pairs={{0,16},{4,20},{8,24},{12,28},{16,0},{20,4},{24,8},{28,12},{1,17},{... | collective-permute-start | bytes 1179656 | tf_op jit(solution)/shard_map/cond/branch_0_fun/ppermute | solution.py:947
  283.0 47.5 %collective-permute-start.11 = (bf16[1536,128]{1,0:T(8,128)(2,1)}, bf16[1536,128]{1,0:T(8,128)(2,1)S(1)}, u32[]{:S(2)}, u32[]{:S(2)}) collective-permute-start(bf16[1536,128]{1,0:T(8,128)(2,1)} %get-tuple-element.138), channel_id=1, source_target_pairs={{0,20},{4,16},{8,28},{12,24},{16,4},{20,0},{24,12},{28,8},{1,21},{... | collective-permute-start | bytes 1179656 | tf_op jit(solution)/shard_map/cond/branch_0_fun/ppermute | solution.py:947
  283.3 79.2 %copy-start.18 = (bf16[1536,128]{1,0:T(8,128)(2,1)}, bf16[1536,128]{1,0:T(8,128)(2,1)S(1)}, u32[]{:S(2)}) copy-start(bf16[1536,128]{1,0:T(8,128)(2,1)S(1)} %collective-permute-done.7.refs_1_) | copy-start | bytes 1179652 | tf_op jit(solution)/shard_map/cond
  283.3 68.5 %collective-permute-start.12 = (bf16[1536,128]{1,0:T(8,128)(2,1)}, bf16[1536,128]{1,0:T(8,128)(2,1)S(1)}, u32[]{:S(2)}, u32[]{:S(2)}) collective-permute-start(bf16[1536,128]{1,0:T(8,128)(2,1)} %get-tuple-element.139), channel_id=1, source_target_pairs={{0,24},{4,28},{8,16},{12,20},{16,8},{20,12},{24,0},{28,4},{1,25},{... | collective-permute-start | bytes 1179656 | tf_op jit(solution)/shard_map/cond/branch_0_fun/ppermute | solution.py:947
  318.7 43.7 %collective-permute-start.13 = (bf16[1536,128]{1,0:T(8,128)(2,1)S(1)}, bf16[1536,128]{1,0:T(8,128)(2,1)S(1)}, u32[]{:S(2)}, u32[]{:S(2)}) collective-permute-start(bf16[1536,128]{1,0:T(8,128)(2,1)S(1)} %copy-done.40), channel_id=1, source_target_pairs={{0,28},{4,24},{8,20},{12,16},{16,12},{20,8},{24,4},{28,0},{1,29},{... | collective-permute-start | bytes 1179656 | tf_op jit(solution)/shard_map/cond/branch_0_fun/ppermute | solution.py:947
  366.6 36.1 %collective-permute-start.14 = (bf16[2056,128]{1,0:T(8,128)(2,1)}, bf16[2056,128]{1,0:T(8,128)(2,1)S(1)}, u32[]{:S(2)}, u32[]{:S(2)}) collective-permute-start(bf16[2056,128]{1,0:T(8,128)(2,1)} %get-tuple-element.141), channel_id=1, source_target_pairs={{0,1},{1,0},{2,3},{3,2},{4,5},{5,4},{6,7},{7,6},{8,9},{9,8},{10,11... | collective-permute-start | bytes 1579016 | tf_op jit(solution)/shard_map/cond/branch_0_fun/ppermute | solution.py:947
  371.4 37.4 %collective-permute-start.15 = (bf16[2056,128]{1,0:T(8,128)(2,1)}, bf16[2056,128]{1,0:T(8,128)(2,1)S(1)}, u32[]{:S(2)}, u32[]{:S(2)}) collective-permute-start(bf16[2056,128]{1,0:T(8,128)(2,1)} %get-tuple-element.142), channel_id=1, source_target_pairs={{0,2},{1,3},{2,0},{3,1},{4,6},{5,7},{6,4},{7,5},{8,10},{9,11},{10,... | collective-permute-start | bytes 1579016 | tf_op jit(solution)/shard_map/cond/branch_0_fun/ppermute | solution.py:947
  371.4 50.6 %collective-permute-start.16 = (bf16[2056,128]{1,0:T(8,128)(2,1)}, bf16[2056,128]{1,0:T(8,128)(2,1)S(1)}, u32[]{:S(2)}, u32[]{:S(2)}) collective-permute-start(bf16[2056,128]{1,0:T(8,128)(2,1)} %get-tuple-element.143), channel_id=1, source_target_pairs={{0,3},{1,2},{2,1},{3,0},{4,7},{5,6},{6,5},{7,4},{8,11},{9,10},{10,... | collective-permute-start | bytes 1579016 | tf_op jit(solution)/shard_map/cond/branch_0_fun/ppermute | solution.py:947
  372.9 1.9 collective-permute-start
  373.6 6.6 %collective-permute-start.1 = (bf16[512,128]{1,0:T(8,128)(2,1)}, bf16[512,128]{1,0:T(8,128)(2,1)S(1)}, u32[]{:S(2)}, u32[]{:S(2)}) collective-permute-start(bf16[512,128]{1,0:T(8,128)(2,1)} %get-tuple-element.124), channel_id=1, source_target_pairs={{0,8},{4,12},{8,0},{12,4},{16,24},{20,28},{24,16},{28,20},{1,9},{5... | collective-permute-start | bytes 393224 | tf_op jit(solution)/shard_map/cond/branch_0_fun/ppermute | solution.py:947
  374.8 6.3 %collective-permute-start.2 = (bf16[512,128]{1,0:T(8,128)(2,1)}, bf16[512,128]{1,0:T(8,128)(2,1)S(1)}, u32[]{:S(2)}, u32[]{:S(2)}) collective-permute-start(bf16[512,128]{1,0:T(8,128)(2,1)} %get-tuple-element.125), channel_id=1, source_target_pairs={{0,12},{4,8},{8,4},{12,0},{16,28},{20,24},{24,20},{28,16},{1,13},{... | collective-permute-start | bytes 393224 | tf_op jit(solution)/shard_map/cond/branch_0_fun/ppermute | solution.py:947
  380.2 7.7 %collective-permute-start.3 = (bf16[512,128]{1,0:T(8,128)(2,1)}, bf16[512,128]{1,0:T(8,128)(2,1)S(1)}, u32[]{:S(2)}, u32[]{:S(2)}) collective-permute-start(bf16[512,128]{1,0:T(8,128)(2,1)} %get-tuple-element.126), channel_id=1, source_target_pairs={{0,16},{4,20},{8,24},{12,28},{16,0},{20,4},{24,8},{28,12},{1,17},{... | collective-permute-start | bytes 393224 | tf_op jit(solution)/shard_map/cond/branch_0_fun/ppermute | solution.py:947
  381.0 7.4 %collective-permute-start.4 = (bf16[512,128]{1,0:T(8,128)(2,1)}, bf16[512,128]{1,0:T(8,128)(2,1)S(1)}, u32[]{:S(2)}, u32[]{:S(2)}) collective-permute-start(bf16[512,128]{1,0:T(8,128)(2,1)} %get-tuple-element.127), channel_id=1, source_target_pairs={{0,20},{4,16},{8,28},{12,24},{16,4},{20,0},{24,12},{28,8},{1,21},{... | collective-permute-start | bytes 393224 | tf_op jit(solution)/shard_map/cond/branch_0_fun/ppermute | solution.py:947
  387.8 7.2 %collective-permute-start.5 = (bf16[512,128]{1,0:T(8,128)(2,1)S(1)}, bf16[512,128]{1,0:T(8,128)(2,1)S(1)}, u32[]{:S(2)}, u32[]{:S(2)}) collective-permute-start(bf16[512,128]{1,0:T(8,128)(2,1)S(1)} %copy-done.47), channel_id=1, source_target_pairs={{0,24},{4,28},{8,16},{12,20},{16,8},{20,12},{24,0},{28,4},{1,25},{... | collective-permute-start | bytes 393224 | tf_op jit(solution)/shard_map/cond/branch_0_fun/ppermute | solution.py:947
  388.4 6.7 %collective-permute-start.6 = (bf16[512,128]{1,0:T(8,128)(2,1)S(1)}, bf16[512,128]{1,0:T(8,128)(2,1)S(1)}, u32[]{:S(2)}, u32[]{:S(2)}) collective-permute-start(bf16[512,128]{1,0:T(8,128)(2,1)S(1)} %copy-done.46), channel_id=1, source_target_pairs={{0,28},{4,24},{8,20},{12,16},{16,12},{20,8},{24,4},{28,0},{1,29},{... | collective-permute-start | bytes 393224 | tf_op jit(solution)/shard_map/cond/branch_0_fun/ppermute | solution.py:947
  (33 other events, 450.6 us)

commit v2 on v1

--- a/solution.py
+++ b/solution.py
@@ -409,6 +409,7 @@
             pltpu.SemaphoreType.DMA((len(panels),)),
         ],
         cost_estimate=pl.CostEstimate(flops=1000, bytes_accessed=8 << 20, transcendentals=0),
+        compiler_params=pltpu.CompilerParams(vmem_limit_bytes=60 << 20),
         name="merge",
     )(*panels)
 
@@ -526,6 +527,7 @@
             pltpu.SemaphoreType.DMA((hops + near_count + 1,)),
         ],
         cost_estimate=pl.CostEstimate(flops=1000, bytes_accessed=4 << 20, transcendentals=0),
+        compiler_params=pltpu.CompilerParams(vmem_limit_bytes=60 << 20),
         name="relay",
     )(*arrived)
 
@@ -588,6 +590,7 @@
             pltpu.SemaphoreType.DMA,
         ],
         cost_estimate=pl.CostEstimate(flops=1000, bytes_accessed=4 << 20, transcendentals=0),
+        compiler_params=pltpu.CompilerParams(vmem_limit_bytes=60 << 20),
         name="relay_back",
     )(places, *arrived)
 
@@ -640,7 +643,6 @@
             pltpu.make_async_copy(ref.at[rows], stage.at[k], in_sem.at[k]).start()
 
     load_t.start()
-    load_n.start()
 
     @pl.loop(0, pairs)
     def _(c):
@@ -664,6 +666,8 @@
         @pl.when(before != 0)
         def _():
             acc[c] = acc[c] + value
+
+    load_n.start()
 
     @pl.loop(0, width)
     def _(a):
@@ -793,8 +797,8 @@
 
 
 def collect_kernel(scale, places, returned, *refs):
-    extras = refs[:-9]
-    fock, energy, listed, parts, result, meta, in_sem, out_sem, meta_sem = refs[-9:]
+    extras = refs[:-10]
+    fock, energy, listed, parts, result, meta, total_e, in_sem, out_sem, meta_sem = refs[-10:]
     owned, copies = parts.shape[:2]
     sources = returned.shape[0]
     meta_in = pltpu.make_async_copy(returned.at[:, meta_rows(returned), :], meta, meta_sem)
@@ -825,7 +829,9 @@
     row = lax.broadcasted_iota(jnp.int32, meta.shape, 1)
     sent = jnp.where((lane < 3) & (row == 0), meta[...].astype(jnp.float32), 0.0)
     per_source = jnp.sum(jnp.sum(sent, axis=0), axis=0, keepdims=True)
-    energy[...] = jnp.sum(per_source, axis=1, keepdims=True) * scale
+    total_e[...] = jnp.sum(per_source, axis=1, keepdims=True) * scale
+    send_e = pltpu.make_async_copy(total_e, energy, meta_sem)
+    send_e.start()
     last = (sources + len(extras)) * LINE
     listed[owned] = 0
 
@@ -852,6 +858,7 @@
         pltpu.make_async_copy(result.at[p], fock.at[p], out_sem).start()
 
     pltpu.make_async_copy(result, fock, out_sem).wait()
+    send_e.wait()
 
 
 def collect_blocks(places, returned, extras, scale, owned, copies):
@@ -864,16 +871,18 @@
             jax.ShapeDtypeStruct((owned + 1,), jnp.int32),
         ),
         in_specs=[smem_spec()] + [any_spec()] * (1 + len(extras)),
-        out_specs=(any_spec(), vmem_spec(), smem_spec()),
+        out_specs=(any_spec(), any_spec(), smem_spec()),
         scratch_shapes=[
             pltpu.VMEM((owned, copies, NBF, NBF), jnp.bfloat16),
             pltpu.VMEM((owned, NBF, NBF), jnp.float32),
             pltpu.VMEM((sources, META, NBF), jnp.bfloat16),
+            pltpu.VMEM((1, 1), jnp.float32),
             pltpu.SemaphoreType.DMA((owned,)),
             pltpu.SemaphoreType.DMA,
             pltpu.SemaphoreType.DMA,
         ],
         cost_estimate=pl.CostEstimate(flops=1000, bytes_accessed=8 << 20, transcendentals=0),
+        compiler_params=pltpu.CompilerParams(vmem_limit_bytes=60 << 20),
         name="collect_blocks",
     )(places, returned, *extras)
 
@@ -933,6 +942,7 @@
             pltpu.SemaphoreType.DMA((owned,)),
             pltpu.SemaphoreType.DMA,
         ],
+        compiler_params=pltpu.CompilerParams(vmem_limit_bytes=60 << 20),
         name="add_blocks",
     )(places, listed, partial, *extras)
 
@@ -977,7 +987,9 @@
     ranks = (rows_z - 1) * (capacity - direct)
     groups = (rows_x, rows_z)
     *panels, places = split_blocks(density, dest, code, direct, groups)
-    lines_in = swap(panels[rows_x:], "gy", 1)
+    lines_in = []
+    for far in reversed(range(1, rows_z)):
+        lines_in = swap([panels[rows_x + far - 1]], "gy", far) + lines_in
     near_in = swap(panels[:rows_x], "gx", 0)
     outgoing = direct_blocks(places, density, domains, direct, copies)
     inbound = exchange(outgoing)

time: 429 us -> 429 us (level)
    unnamed x47 -> x51, local copies, waits for them, and re-layouts: 10.6 us -> 10.6 us
  transfers between devices with their start and end apart: 36 -> 36, of which waited for: 20 -> 21; matrix products, arithmetic and copies ran while one was open for 2% -> 2% of each run, Pallas kernels for 5% -> 5%
where the time goes in v2:
time: 429 us; the launch traced here: 428 us
  waiting for transfers between devices  290 us (68%)
  Pallas kernels  73.9 us (17%)
  starting transfers between devices  47.9 us (11%)
  local copies, waits for them, and re-layouts  12.8 us (3%)
    ppermute x34, waiting for transfers between devices, swap(): lax.ppermute(array, axis, [(i, i ^ first + k) for i in range(size)])  290 us
    pallas_call x1, Pallas kernels, domain_build(): pl.pallas_call(functools.partial(domain_kernel, len(extras)), out_shape=t...  39.1 us
    ppermute x34, starting transfers between devices, swap(): lax.ppermute(array, axis, [(i, i ^ first + k) for i in range(size)])  32 us
    all_to_all x2, starting transfers between devices, exchange(): return lax.all_to_all(array, AXES, split_axis=0, concat_axis=0, tiled=True)  15.9 us
    unnamed x51, local copies, waits for them, and re-layouts  10.6 us
  transfers between devices with their start and end apart: 36, of which 21 were waited for; matrix products, arithmetic and copies ran while one was open for 2% of the time, Pallas kernels for 5%

profile of v2, /device:TPU:8, one launch (start us, length us, event | category | flops | bytes accessed | tf_op | source)
XLA Modules:
  0.0 428.2 jit_solution(10820392506430015312)
XLA Ops:
  0.6 4.3 %split_blocks.1 = (bf16[520,128]{1,0:T(8,128)(2,1)}, bf16[520,128]{1,0:T(8,128)(2,1)}, bf16[520,128]{1,0:T(8,128)(2,1)}, bf16[520,128]{1,0:T(8,128)(2,1)}, bf16[...) custom-call(s32[2,64]{1,0:T(2,128)} %bitcast.21, ...), custom_call_target="tpu_custom_call" | custom-call | tf_op jit(solution)/shard_map/split_blocks/pallas_call | solution.py:217
  5.0 4.0 direct_blocks.3
  9.1 6.2 %all-to-all-start.4 = ((bf16[32,512,128]{2,1,0:T(8,128)(2,1)}), bf16[32,512,128]{2,1,0:T(8,128)(2,1)}, u32[]{:S(2)}, u32[]{:S(2)}) async-start(bf16[32,512,128]{2,1,0:T(8,128)(2,1)} %direct_blocks.3), calls=%async_computation.4 | async-start | bytes 8388608 | tf_op jit(solution)/shard_map/all_to_all | solution.py:951
  15.7 2.6 collective-permute-start.25
  18.9 77.9 %collective-permute-done.24.refs_0_ = bf16[2056,128]{1,0:T(8,128)(2,1)S(1)} collective-permute-done((bf16[2056,128]{1,0:T(8,128)(2,1)S(1)}, bf16[2056,128]{1,0:T(8,128)(2,1)S(1)}, u32[]{:S(2)}, u32[]{:S(2)}) %collective-permute-start.24) | collective-permute-done | bytes 526368 | tf_op jit(solution)/shard_map/ppermute | solution.py:957
  96.8 44.6 %collective-permute-done.25.refs_1_ = bf16[2056,128]{1,0:T(8,128)(2,1)S(1)} collective-permute-done((bf16[2056,128]{1,0:T(8,128)(2,1)S(1)}, bf16[2056,128]{1,0:T(8,128)(2,1)S(1)}, u32[]{:S(2)}, u32[]{:S(2)}) %collective-permute-start.25) | collective-permute-done | bytes 526368 | tf_op jit(solution)/shard_map/ppermute | solution.py:957
  141.4 13.5 %collective-permute-done.26.refs_2_ = bf16[2056,128]{1,0:T(8,128)(2,1)S(1)} collective-permute-done((bf16[2056,128]{1,0:T(8,128)(2,1)S(1)}, bf16[2056,128]{1,0:T(8,128)(2,1)S(1)}, u32[]{:S(2)}, u32[]{:S(2)}) %collective-permute-start.26) | collective-permute-done | bytes 526368 | tf_op jit(solution)/shard_map/ppermute | solution.py:957
  155.7 6.9 %relay.1 = (bf16[1544,128]{1,0:T(8,128)(2,1)}, bf16[1544,128]{1,0:T(8,128)(2,1)}, bf16[1544,128]{1,0:T(8,128)(2,1)}, bf16[1544,128]{1,0:T(8,128)(2,1)}, bf16[154...) custom-call(bf16[2056,128]{1,0:T(8,128)(2,1)} %copy-done.15, ...), custom_call_target="tpu_custom_call" | custom-call | flops 1000 | bytes 4194304 | tf_op jit(solution)/shard_map/relay/pallas_call | solution.py:512
  162.8 2.0 collective-permute-start.18
  164.8 1.6 collective-permute-start.20
  166.4 11.5 %collective-permute-done.18.refs_2_ = bf16[520,128]{1,0:T(8,128)(2,1)S(1)} collective-permute-done((bf16[520,128]{1,0:T(8,128)(2,1)}, bf16[520,128]{1,0:T(8,128)(2,1)S(1)}, u32[]{:S(2)}, u32[]{:S(2)}) %collective-permute-start.18) | collective-permute-done | bytes 133152 | tf_op jit(solution)/shard_map/ppermute | solution.py:957
  178.0 1.6 collective-permute-done.19.refs_3_
  179.7 1.5 collective-permute-start.22
  181.1 1.2 collective-permute-start.23
  182.3 6.6 %collective-permute-done.21.refs_5_ = bf16[520,128]{1,0:T(8,128)(2,1)S(1)} collective-permute-done((bf16[520,128]{1,0:T(8,128)(2,1)S(1)}, bf16[520,128]{1,0:T(8,128)(2,1)S(1)}, u32[]{:S(2)}, u32[]{:S(2)}) %collective-permute-start.21) | collective-permute-done | bytes 133152 | tf_op jit(solution)/shard_map/ppermute | solution.py:957
  189.0 1.4 collective-permute-start.31
  190.5 1.7 collective-permute-start.32
  192.2 1.2 collective-permute-start.33
  193.7 8.6 %copy.17 = bf16[2048,1536]{0,1:T(8,128)(2,1)} copy(bf16[2048,1536]{1,0:T(8,128)(2,1)} %param.15) | data formatting | bytes 12582912 | tf_op args[3]
  202.4 1.0 fusion
  203.4 14.8 %collective-permute-done.30.refs_12_ = bf16[1544,128]{1,0:T(8,128)(2,1)} collective-permute-done((bf16[1544,128]{1,0:T(8,128)(2,1)}, bf16[1544,128]{1,0:T(8,128)(2,1)}, u32[]{:S(2)}, u32[]{:S(2)}) %collective-permute-start.30) | collective-permute-done | bytes 395296 | tf_op jit(solution)/shard_map/ppermute | solution.py:957
  218.3 6.8 %collective-permute-done.31.refs_13_ = bf16[1544,128]{1,0:T(8,128)(2,1)} collective-permute-done((bf16[1544,128]{1,0:T(8,128)(2,1)}, bf16[1544,128]{1,0:T(8,128)(2,1)}, u32[]{:S(2)}, u32[]{:S(2)}) %collective-permute-start.31) | collective-permute-done | bytes 395296 | tf_op jit(solution)/shard_map/ppermute | solution.py:957
  225.0 4.9 %merge.1 = (s32[18]{0:T(128)S(1)}, s32[256]{0:T(256)S(1)}, s32[256]{0:T(256)S(1)}, s32[1]{0:T(128)}) custom-call(bf16[520,128]{1,0:T(8,128)(2,1)} %get-tuple-element.192.refs_0_, bf16[520,128]{1,0:T(8,128)(2,1)} %copy-done.5, bf16[520,128]{1,0:T(8,128)(2,1)} %copy-done.6, bf16[520,128]{1,0:T(8,128)(2,1)} %copy-done.7, bf16[520,128]{1,0:T(8,128)(2,1)} %copy-done.8, ...), custom_call_target="tpu_custom_call" | custom-call | flops 1000 | bytes 8388608 | tf_op jit(solution)/shard_map/merge/pallas_call | solution.py:394
  230.7 196.6 %conditional.1 = (f32[64,128,128]{2,1,0:T(8,128)}, f32[]{:T(128)}) conditional(s32[]{:T(128)} %bitcast.6, (s32[18]{0:T(128)S(1)}, s32[256]{0:T(256)S(1)}, s32[256]{0:T(256)S(1)}, bf16[32,512,128]{2,1,0:T(8,128)(2,1)}, bf16[520,128]{1,0:T(8,128)(2,1)}, /*index=5*/bf16[520,128]{1,0:T(8,128)(2,1)}, bf16[520,128]{1,0:T(8,128)(2,1)}, ...), branch_computations={%region_0.0_spmd, %region_1.0_spmd} | conditional | flops 3000 | bytes 75221080 | solution.py:1009
  230.7 39.1 %domain_build.2 = (bf16[32,520,128]{2,1,0:T(8,128)(2,1)}, bf16[512,128]{1,0:T(8,128)(2,1)}, bf16[512,128]{1,0:T(8,128)(2,1)}, bf16[512,128]{1,0:T(8,128)(2,1)}, ...) custom-call(s32[18]{0:T(128)S(1)} %get-tuple-element.91.starts, ...), custom_call_target="tpu_custom_call" | custom-call | tf_op jit(solution)/shard_map/cond/branch_0_fun/domain_build/pallas_call | solution.py:770
  269.8 9.7 %all-to-all-start = ((bf16[32,520,128]{2,1,0:T(8,128)(2,1)}), bf16[32,520,128]{2,1,0:T(8,128)(2,1)}, u32[]{:S(2)}, u32[]{:S(2)}) async-start(bf16[32,520,128]{2,1,0:T(8,128)(2,1)} %get-tuple-element.121), calls=%async_computation | async-start | bytes 8519680 | tf_op jit(solution)/shard_map/cond/branch_0_fun/all_to_all | solution.py:951
  279.8 1.5 collective-permute-start.8
  281.5 1.5 collective-permute-start.10
  283.3 2.4 collective-permute-start.12
  285.7 33.0 %collective-permute-done.8.refs_2_ = bf16[1536,128]{1,0:T(8,128)(2,1)S(1)} collective-permute-done((bf16[1536,128]{1,0:T(8,128)(2,1)S(1)}, bf16[1536,128]{1,0:T(8,128)(2,1)S(1)}, u32[]{:S(2)}, u32[]{:S(2)}) %collective-permute-start.8) | collective-permute-done | bytes 393248 | tf_op jit(solution)/shard_map/cond/branch_0_fun/ppermute | solution.py:957
  319.0 11.5 %collective-permute-done.9.refs_3_ = bf16[1536,128]{1,0:T(8,128)(2,1)S(1)} collective-permute-done((bf16[1536,128]{1,0:T(8,128)(2,1)}, bf16[1536,128]{1,0:T(8,128)(2,1)S(1)}, u32[]{:S(2)}, u32[]{:S(2)}) %collective-permute-start.9) | collective-permute-done | bytes 393248 | tf_op jit(solution)/shard_map/cond/branch_0_fun/ppermute | solution.py:957
  330.5 21.3 %collective-permute-done.12.refs_6_ = bf16[1536,128]{1,0:T(8,128)(2,1)S(1)} collective-permute-done((bf16[1536,128]{1,0:T(8,128)(2,1)S(1)}, bf16[1536,128]{1,0:T(8,128)(2,1)S(1)}, u32[]{:S(2)}, u32[]{:S(2)}) %collective-permute-start.12) | collective-permute-done | bytes 393248 | tf_op jit(solution)/shard_map/cond/branch_0_fun/ppermute | solution.py:957
  351.8 10.6 %collective-permute-done.13.refs_7_ = bf16[1536,128]{1,0:T(8,128)(2,1)S(1)} collective-permute-done((bf16[1536,128]{1,0:T(8,128)(2,1)S(1)}, bf16[1536,128]{1,0:T(8,128)(2,1)S(1)}, u32[]{:S(2)}, u32[]{:S(2)}) %collective-permute-start.13) | collective-permute-done | bytes 393248 | tf_op jit(solution)/shard_map/cond/branch_0_fun/ppermute | solution.py:957
  363.2 3.4 relay_back.1
  366.6 4.7 %collective-permute-start.14 = (bf16[2056,128]{1,0:T(8,128)(2,1)}, bf16[2056,128]{1,0:T(8,128)(2,1)S(1)}, u32[]{:S(2)}, u32[]{:S(2)}) collective-permute-start(bf16[2056,128]{1,0:T(8,128)(2,1)} %get-tuple-element.141), channel_id=1, source_target_pairs={{0,1},{1,0},{2,3},{3,2},{4,5},{5,4},{6,7},{7,6},{8,9},{9,8},{10,11... | collective-permute-start | bytes 1579016 | tf_op jit(solution)/shard_map/cond/branch_0_fun/ppermute | solution.py:957
  371.3 1.5 collective-permute-start.16
  373.6 1.2 collective-permute-done.refs_1_
  374.9 5.2 %collective-permute-done.1.refs_2_ = bf16[512,128]{1,0:T(8,128)(2,1)S(1)} collective-permute-done((bf16[512,128]{1,0:T(8,128)(2,1)}, bf16[512,128]{1,0:T(8,128)(2,1)S(1)}, u32[]{:S(2)}, u32[]{:S(2)}) %collective-permute-start.1) | collective-permute-done | bytes 131104 | tf_op jit(solution)/shard_map/cond/branch_0_fun/ppermute | solution.py:957
  381.0 1.5 collective-permute-start.4
  382.5 3.9 collective-permute-done.3.refs_4_
  386.4 2.0 collective-permute-done.4.refs_5_
  388.4 1.7 collective-permute-start.6
  390.2 2.4 collective-permute-done.5.refs_6_
  392.5 1.4 collective-permute-done.6.refs_7_
  394.6 6.9 %collect_blocks.2 = (f32[64,128,128]{2,1,0:T(8,128)}, f32[1,1]{1,0:T(1,128)}, s32[65]{0:T(128)}) custom-call(s32[8,128]{1,0:T(8,128)S(1)} %get-tuple-element.90.places, bf16[32,520,128]{2,1,0:T(8,128)(2,1)} %all-to-all-done.returned, bf16[512,128]{1,0:T(8,128)(2,1)} %get-tuple-element.122.refs_0_, bf16[512,128]{1,0:T(8,128)(2,1)} %copy-done.26, ...), custom_call_target="tpu_custom_call" | custom-call | flops 1000 | bytes 8388608 | tf_op jit(solution)/shard_map/cond/branch_0_fun/collect_blocks/pallas_call | solution.py:866
  401.5 7.3 %collective-permute-done.15.refs_1_ = bf16[2056,128]{1,0:T(8,128)(2,1)S(1)} collective-permute-done((bf16[2056,128]{1,0:T(8,128)(2,1)}, bf16[2056,128]{1,0:T(8,128)(2,1)S(1)}, u32[]{:S(2)}, u32[]{:S(2)}) %collective-permute-start.15) | collective-permute-done | bytes 526368 | tf_op jit(solution)/shard_map/cond/branch_0_fun/ppermute | solution.py:957
  408.8 13.2 %collective-permute-done.16.refs_2_ = bf16[2056,128]{1,0:T(8,128)(2,1)S(1)} collective-permute-done((bf16[2056,128]{1,0:T(8,128)(2,1)}, bf16[2056,128]{1,0:T(8,128)(2,1)S(1)}, u32[]{:S(2)}, u32[]{:S(2)}) %collective-permute-start.16) | collective-permute-done | bytes 526368 | tf_op jit(solution)/shard_map/cond/branch_0_fun/ppermute | solution.py:957
  422.7 4.3 add_blocks.1
  (131 shorter events, 8.2 us)
Async XLA Ops:
  0.6 201.7 %copy-start = (f32[10,2048]{1,0:T(8,128)S(1)}, f32[10,2048]{1,0:T(8,128)}, u32[]{:S(2)}) copy-start(f32[10,2048]{1,0:T(8,128)} %param.16) | copy-start | bytes 245764
  9.1 155.7 %copy-start.49 = (bf16[520,128]{1,0:T(8,128)(2,1)S(1)}, bf16[520,128]{1,0:T(8,128)(2,1)}, u32[]{:S(2)}) copy-start(bf16[520,128]{1,0:T(8,128)(2,1)} %get-tuple-element.196) | copy-start | bytes 399364
  9.1 168.8 %copy-start.48 = (bf16[520,128]{1,0:T(8,128)(2,1)S(1)}, bf16[520,128]{1,0:T(8,128)(2,1)}, u32[]{:S(2)}) copy-start(bf16[520,128]{1,0:T(8,128)(2,1)} %get-tuple-element.197) | copy-start | bytes 399364
  9.1 170.6 %copy-start.47 = (bf16[520,128]{1,0:T(8,128)(2,1)S(1)}, bf16[520,128]{1,0:T(8,128)(2,1)}, u32[]{:S(2)}) copy-start(bf16[520,128]{1,0:T(8,128)(2,1)} %get-tuple-element.198) | copy-start | bytes 399364
  9.1 172.0 %copy-start.46 = (bf16[520,128]{1,0:T(8,128)(2,1)S(1)}, bf16[520,128]{1,0:T(8,128)(2,1)}, u32[]{:S(2)}) copy-start(bf16[520,128]{1,0:T(8,128)(2,1)} %get-tuple-element.199) | copy-start | bytes 399364
  9.1 184.4 %copy-start.3 = (f32[128,128]{1,0:T(8,128)S(1)}, f32[128,128]{1,0:T(8,128)}, u32[]{:S(2)}) copy-start(f32[128,128]{1,0:T(8,128)} %param.19) | copy-start | bytes 196612
  9.1 184.5 %copy-start.4 = (f32[128,128]{1,0:T(8,128)S(1)}, f32[128,128]{1,0:T(8,128)}, u32[]{:S(2)}) copy-start(f32[128,128]{1,0:T(8,128)} %param.20) | copy-start | bytes 196612
  9.1 221.5 %all-to-all-start.4 = ((bf16[32,512,128]{2,1,0:T(8,128)(2,1)}), bf16[32,512,128]{2,1,0:T(8,128)(2,1)}, u32[]{:S(2)}, u32[]{:S(2)}) async-start(bf16[32,512,128]{2,1,0:T(8,128)(2,1)} %direct_blocks.3), calls=%async_computation.4 | async-start | bytes 8388608 | tf_op jit(solution)/shard_map/all_to_all | solution.py:951
  15.3 81.4 %collective-permute-start.24 = (bf16[2056,128]{1,0:T(8,128)(2,1)S(1)}, bf16[2056,128]{1,0:T(8,128)(2,1)S(1)}, u32[]{:S(2)}, u32[]{:S(2)}) collective-permute-start(bf16[2056,128]{1,0:T(8,128)(2,1)S(1)} %copy-done.40), channel_id=1, source_target_pairs={{0,1},{1,0},{2,3},{3,2},{4,5},{5,4},{6,7},{7,6},{8,9},{9,8},{10,11... | collective-permute-start | bytes 1579016 | tf_op jit(solution)/shard_map/ppermute | solution.py:957
  15.7 125.6 %collective-permute-start.25 = (bf16[2056,128]{1,0:T(8,128)(2,1)S(1)}, bf16[2056,128]{1,0:T(8,128)(2,1)S(1)}, u32[]{:S(2)}, u32[]{:S(2)}) collective-permute-start(bf16[2056,128]{1,0:T(8,128)(2,1)S(1)} %copy-done.39), channel_id=1, source_target_pairs={{0,2},{1,3},{2,0},{3,1},{4,6},{5,7},{6,4},{7,5},{8,10},{9,11},{10,... | collective-permute-start | bytes 1579016 | tf_op jit(solution)/shard_map/ppermute | solution.py:957
  18.3 136.6 %collective-permute-start.26 = (bf16[2056,128]{1,0:T(8,128)(2,1)S(1)}, bf16[2056,128]{1,0:T(8,128)(2,1)S(1)}, u32[]{:S(2)}, u32[]{:S(2)}) collective-permute-start(bf16[2056,128]{1,0:T(8,128)(2,1)S(1)} %copy-done.38), channel_id=1, source_target_pairs={{0,3},{1,2},{2,1},{3,0},{4,7},{5,6},{6,5},{7,4},{8,11},{9,10},{10,... | collective-permute-start | bytes 1579016 | tf_op jit(solution)/shard_map/ppermute | solution.py:957
  18.9 145.9 %collective-permute-start.17 = (bf16[520,128]{1,0:T(8,128)(2,1)}, bf16[520,128]{1,0:T(8,128)(2,1)S(1)}, u32[]{:S(2)}, u32[]{:S(2)}) collective-permute-start(bf16[520,128]{1,0:T(8,128)(2,1)} %get-tuple-element.193), channel_id=1, source_target_pairs={{0,4},{4,0},{8,12},{12,8},{16,20},{20,16},{24,28},{28,24},{1,5},{5... | collective-permute-start | bytes 399368 | tf_op jit(solution)/shard_map/ppermute | solution.py:957
  96.8 58.2 %copy-start.15 = (bf16[2056,128]{1,0:T(8,128)(2,1)}, bf16[2056,128]{1,0:T(8,128)(2,1)S(1)}, u32[]{:S(2)}) copy-start(bf16[2056,128]{1,0:T(8,128)(2,1)S(1)} %collective-permute-done.24.refs_0_) | copy-start | bytes 1579012
  162.6 27.8 %collective-permute-start.27 = (bf16[1544,128]{1,0:T(8,128)(2,1)}, bf16[1544,128]{1,0:T(8,128)(2,1)}, u32[]{:S(2)}, u32[]{:S(2)}) collective-permute-start(bf16[1544,128]{1,0:T(8,128)(2,1)} %get-tuple-element.204), channel_id=1, source_target_pairs={{0,4},{4,0},{8,12},{12,8},{16,20},{20,16},{24,28},{28,24},{1,5},{5... | collective-permute-start | bytes 1185800 | tf_op jit(solution)/shard_map/ppermute | solution.py:957
  162.7 29.5 %collective-permute-start.28 = (bf16[1544,128]{1,0:T(8,128)(2,1)}, bf16[1544,128]{1,0:T(8,128)(2,1)}, u32[]{:S(2)}, u32[]{:S(2)}) collective-permute-start(bf16[1544,128]{1,0:T(8,128)(2,1)} %get-tuple-element.205), channel_id=1, source_target_pairs={{0,8},{4,12},{8,0},{12,4},{16,24},{20,28},{24,16},{28,20},{1,9},{5... | collective-permute-start | bytes 1185800 | tf_op jit(solution)/shard_map/ppermute | solution.py:957
  162.8 15.1 %collective-permute-start.18 = (bf16[520,128]{1,0:T(8,128)(2,1)}, bf16[520,128]{1,0:T(8,128)(2,1)S(1)}, u32[]{:S(2)}, u32[]{:S(2)}) collective-permute-start(bf16[520,128]{1,0:T(8,128)(2,1)} %get-tuple-element.194), channel_id=1, source_target_pairs={{0,8},{4,12},{8,0},{12,4},{16,24},{20,28},{24,16},{28,20},{1,9},{5... | collective-permute-start | bytes 399368 | tf_op jit(solution)/shard_map/ppermute | solution.py:957
  164.8 14.8 %collective-permute-start.19 = (bf16[520,128]{1,0:T(8,128)(2,1)}, bf16[520,128]{1,0:T(8,128)(2,1)S(1)}, u32[]{:S(2)}, u32[]{:S(2)}) collective-permute-start(bf16[520,128]{1,0:T(8,128)(2,1)} %get-tuple-element.195), channel_id=1, source_target_pairs={{0,12},{4,8},{8,4},{12,0},{16,28},{20,24},{24,20},{28,16},{1,13},{... | collective-permute-start | bytes 399368 | tf_op jit(solution)/shard_map/ppermute | solution.py:957
  164.8 16.3 %collective-permute-start.20 = (bf16[520,128]{1,0:T(8,128)(2,1)S(1)}, bf16[520,128]{1,0:T(8,128)(2,1)S(1)}, u32[]{:S(2)}, u32[]{:S(2)}) collective-permute-start(bf16[520,128]{1,0:T(8,128)(2,1)S(1)} %copy-done.49), channel_id=1, source_target_pairs={{0,16},{4,20},{8,24},{12,28},{16,0},{20,4},{24,8},{28,12},{1,17},{... | collective-permute-start | bytes 399368 | tf_op jit(solution)/shard_map/ppermute | solution.py:957
  177.9 11.0 %collective-permute-start.21 = (bf16[520,128]{1,0:T(8,128)(2,1)S(1)}, bf16[520,128]{1,0:T(8,128)(2,1)S(1)}, u32[]{:S(2)}, u32[]{:S(2)}) collective-permute-start(bf16[520,128]{1,0:T(8,128)(2,1)S(1)} %copy-done.48), channel_id=1, source_target_pairs={{0,20},{4,16},{8,28},{12,24},{16,4},{20,0},{24,12},{28,8},{1,21},{... | collective-permute-start | bytes 399368 | tf_op jit(solution)/shard_map/ppermute | solution.py:957
  179.7 9.3 %collective-permute-start.22 = (bf16[520,128]{1,0:T(8,128)(2,1)S(1)}, bf16[520,128]{1,0:T(8,128)(2,1)S(1)}, u32[]{:S(2)}, u32[]{:S(2)}) collective-permute-start(bf16[520,128]{1,0:T(8,128)(2,1)S(1)} %copy-done.47), channel_id=1, source_target_pairs={{0,24},{4,28},{8,16},{12,20},{16,8},{20,12},{24,0},{28,4},{1,25},{... | collective-permute-start | bytes 399368 | tf_op jit(solution)/shard_map/ppermute | solution.py:957
  181.1 7.9 %collective-permute-start.23 = (bf16[520,128]{1,0:T(8,128)(2,1)S(1)}, bf16[520,128]{1,0:T(8,128)(2,1)S(1)}, u32[]{:S(2)}, u32[]{:S(2)}) collective-permute-start(bf16[520,128]{1,0:T(8,128)(2,1)S(1)} %copy-done.46), channel_id=1, source_target_pairs={{0,28},{4,24},{8,20},{12,16},{16,12},{20,8},{24,4},{28,0},{1,29},{... | collective-permute-start | bytes 399368 | tf_op jit(solution)/shard_map/ppermute | solution.py:957
  188.9 14.5 %collective-permute-start.29 = (bf16[1544,128]{1,0:T(8,128)(2,1)}, bf16[1544,128]{1,0:T(8,128)(2,1)}, u32[]{:S(2)}, u32[]{:S(2)}) collective-permute-start(bf16[1544,128]{1,0:T(8,128)(2,1)} %get-tuple-element.206), channel_id=1, source_target_pairs={{0,12},{4,8},{8,4},{12,0},{16,28},{20,24},{24,20},{28,16},{1,13},{... | collective-permute-start | bytes 1185800 | tf_op jit(solution)/shard_map/ppermute | solution.py:957
  188.9 29.4 %collective-permute-start.30 = (bf16[1544,128]{1,0:T(8,128)(2,1)}, bf16[1544,128]{1,0:T(8,128)(2,1)}, u32[]{:S(2)}, u32[]{:S(2)}) collective-permute-start(bf16[1544,128]{1,0:T(8,128)(2,1)} %get-tuple-element.207), channel_id=1, source_target_pairs={{0,16},{4,20},{8,24},{12,28},{16,0},{20,4},{24,8},{28,12},{1,17},{... | collective-permute-start | bytes 1185800 | tf_op jit(solution)/shard_map/ppermute | solution.py:957
  189.0 36.0 %collective-permute-start.31 = (bf16[1544,128]{1,0:T(8,128)(2,1)}, bf16[1544,128]{1,0:T(8,128)(2,1)}, u32[]{:S(2)}, u32[]{:S(2)}) collective-permute-start(bf16[1544,128]{1,0:T(8,128)(2,1)} %get-tuple-element.208), channel_id=1, source_target_pairs={{0,20},{4,16},{8,28},{12,24},{16,4},{20,0},{24,12},{28,8},{1,21},{... | collective-permute-start | bytes 1185800 | tf_op jit(solution)/shard_map/ppermute | solution.py:957
  190.5 34.6 %collective-permute-start.32 = (bf16[1544,128]{1,0:T(8,128)(2,1)}, bf16[1544,128]{1,0:T(8,128)(2,1)}, u32[]{:S(2)}, u32[]{:S(2)}) collective-permute-start(bf16[1544,128]{1,0:T(8,128)(2,1)} %get-tuple-element.209), channel_id=1, source_target_pairs={{0,24},{4,28},{8,16},{12,20},{16,8},{20,12},{24,0},{28,4},{1,25},{... | collective-permute-start | bytes 1185800 | tf_op jit(solution)/shard_map/ppermute | solution.py:957
  192.2 32.8 %collective-permute-start.33 = (bf16[1544,128]{1,0:T(8,128)(2,1)}, bf16[1544,128]{1,0:T(8,128)(2,1)}, u32[]{:S(2)}, u32[]{:S(2)}) collective-permute-start(bf16[1544,128]{1,0:T(8,128)(2,1)} %get-tuple-element.210), channel_id=1, source_target_pairs={{0,28},{4,24},{8,20},{12,16},{16,12},{20,8},{24,4},{28,0},{1,29},{... | collective-permute-start | bytes 1185800 | tf_op jit(solution)/shard_map/ppermute | solution.py:957
  269.8 48.9 %copy-start.41 = (bf16[1536,128]{1,0:T(8,128)(2,1)S(1)}, bf16[1536,128]{1,0:T(8,128)(2,1)}, u32[]{:S(2)}) copy-start(bf16[1536,128]{1,0:T(8,128)(2,1)} %get-tuple-element.140) | copy-start | bytes 1179652 | tf_op jit(solution)/shard_map/cond
  269.8 93.3 %copy-start.37 = (s32[3,16]{1,0:T(4,128)S(1)}, s32[3,16]{1,0:T(4,128)}, u32[]{:S(2)}) copy-start(s32[3,16]{1,0:T(4,128)} %get-tuple-element.132.places) | copy-start | bytes 580 | tf_op jit(solution)/shard_map/cond
  269.8 124.1 %all-to-all-start = ((bf16[32,520,128]{2,1,0:T(8,128)(2,1)}), bf16[32,520,128]{2,1,0:T(8,128)(2,1)}, u32[]{:S(2)}, u32[]{:S(2)}) async-start(bf16[32,520,128]{2,1,0:T(8,128)(2,1)} %get-tuple-element.121), calls=%async_computation | async-start | bytes 8519680 | tf_op jit(solution)/shard_map/cond/branch_0_fun/all_to_all | solution.py:951
  279.6 3.7 collective-permute-start.7
  279.8 39.0 %collective-permute-start.8 = (bf16[1536,128]{1,0:T(8,128)(2,1)S(1)}, bf16[1536,128]{1,0:T(8,128)(2,1)S(1)}, u32[]{:S(2)}, u32[]{:S(2)}) collective-permute-start(bf16[1536,128]{1,0:T(8,128)(2,1)S(1)} %copy-done.44), channel_id=1, source_target_pairs={{0,8},{4,12},{8,0},{12,4},{16,24},{20,28},{24,16},{28,20},{1,9},{5... | collective-permute-start | bytes 1179656 | tf_op jit(solution)/shard_map/cond/branch_0_fun/ppermute | solution.py:957
  281.2 49.2 %collective-permute-start.9 = (bf16[1536,128]{1,0:T(8,128)(2,1)}, bf16[1536,128]{1,0:T(8,128)(2,1)S(1)}, u32[]{:S(2)}, u32[]{:S(2)}) collective-permute-start(bf16[1536,128]{1,0:T(8,128)(2,1)} %get-tuple-element.136), channel_id=1, source_target_pairs={{0,12},{4,8},{8,4},{12,0},{16,28},{20,24},{24,20},{28,16},{1,13},{... | collective-permute-start | bytes 1179656 | tf_op jit(solution)/shard_map/cond/branch_0_fun/ppermute | solution.py:957
  281.5 49.0 %collective-permute-start.10 = (bf16[1536,128]{1,0:T(8,128)(2,1)}, bf16[1536,128]{1,0:T(8,128)(2,1)S(1)}, u32[]{:S(2)}, u32[]{:S(2)}) collective-permute-start(bf16[1536,128]{1,0:T(8,128)(2,1)} %get-tuple-element.137), channel_id=1, source_target_pairs={{0,16},{4,20},{8,24},{12,28},{16,0},{20,4},{24,8},{28,12},{1,17},{... | collective-permute-start | bytes 1179656 | tf_op jit(solution)/shard_map/cond/branch_0_fun/ppermute | solution.py:957
  283.0 47.5 %collective-permute-start.11 = (bf16[1536,128]{1,0:T(8,128)(2,1)S(1)}, bf16[1536,128]{1,0:T(8,128)(2,1)S(1)}, u32[]{:S(2)}, u32[]{:S(2)}) collective-permute-start(bf16[1536,128]{1,0:T(8,128)(2,1)S(1)} %copy-done.43), channel_id=1, source_target_pairs={{0,20},{4,16},{8,28},{12,24},{16,4},{20,0},{24,12},{28,8},{1,21},{... | collective-permute-start | bytes 1179656 | tf_op jit(solution)/shard_map/cond/branch_0_fun/ppermute | solution.py:957
  283.3 79.2 %copy-start.18 = (bf16[1536,128]{1,0:T(8,128)(2,1)}, bf16[1536,128]{1,0:T(8,128)(2,1)S(1)}, u32[]{:S(2)}) copy-start(bf16[1536,128]{1,0:T(8,128)(2,1)S(1)} %collective-permute-done.7.refs_1_) | copy-start | bytes 1179652 | tf_op jit(solution)/shard_map/cond
  283.3 68.5 %collective-permute-start.12 = (bf16[1536,128]{1,0:T(8,128)(2,1)S(1)}, bf16[1536,128]{1,0:T(8,128)(2,1)S(1)}, u32[]{:S(2)}, u32[]{:S(2)}) collective-permute-start(bf16[1536,128]{1,0:T(8,128)(2,1)S(1)} %copy-done.42), channel_id=1, source_target_pairs={{0,24},{4,28},{8,16},{12,20},{16,8},{20,12},{24,0},{28,4},{1,25},{... | collective-permute-start | bytes 1179656 | tf_op jit(solution)/shard_map/cond/branch_0_fun/ppermute | solution.py:957
  318.7 43.7 %copy-start.19 = (bf16[1536,128]{1,0:T(8,128)(2,1)}, bf16[1536,128]{1,0:T(8,128)(2,1)S(1)}, u32[]{:S(2)}) copy-start(bf16[1536,128]{1,0:T(8,128)(2,1)S(1)} %collective-permute-done.8.refs_2_) | copy-start | bytes 1179652 | tf_op jit(solution)/shard_map/cond
  318.7 43.7 %collective-permute-start.13 = (bf16[1536,128]{1,0:T(8,128)(2,1)S(1)}, bf16[1536,128]{1,0:T(8,128)(2,1)S(1)}, u32[]{:S(2)}, u32[]{:S(2)}) collective-permute-start(bf16[1536,128]{1,0:T(8,128)(2,1)S(1)} %copy-done.41), channel_id=1, source_target_pairs={{0,28},{4,24},{8,20},{12,16},{16,12},{20,8},{24,4},{28,0},{1,29},{... | collective-permute-start | bytes 1179656 | tf_op jit(solution)/shard_map/cond/branch_0_fun/ppermute | solution.py:957
  366.6 34.9 %collective-permute-start.14 = (bf16[2056,128]{1,0:T(8,128)(2,1)}, bf16[2056,128]{1,0:T(8,128)(2,1)S(1)}, u32[]{:S(2)}, u32[]{:S(2)}) collective-permute-start(bf16[2056,128]{1,0:T(8,128)(2,1)} %get-tuple-element.141), channel_id=1, source_target_pairs={{0,1},{1,0},{2,3},{3,2},{4,5},{5,4},{6,7},{7,6},{8,9},{9,8},{10,11... | collective-permute-start | bytes 1579016 | tf_op jit(solution)/shard_map/cond/branch_0_fun/ppermute | solution.py:957
  371.3 37.4 %collective-permute-start.15 = (bf16[2056,128]{1,0:T(8,128)(2,1)}, bf16[2056,128]{1,0:T(8,128)(2,1)S(1)}, u32[]{:S(2)}, u32[]{:S(2)}) collective-permute-start(bf16[2056,128]{1,0:T(8,128)(2,1)} %get-tuple-element.142), channel_id=1, source_target_pairs={{0,2},{1,3},{2,0},{3,1},{4,6},{5,7},{6,4},{7,5},{8,10},{9,11},{10,... | collective-permute-start | bytes 1579016 | tf_op jit(solution)/shard_map/cond/branch_0_fun/ppermute | solution.py:957
  371.3 50.6 %collective-permute-start.16 = (bf16[2056,128]{1,0:T(8,128)(2,1)}, bf16[2056,128]{1,0:T(8,128)(2,1)S(1)}, u32[]{:S(2)}, u32[]{:S(2)}) collective-permute-start(bf16[2056,128]{1,0:T(8,128)(2,1)} %get-tuple-element.143), channel_id=1, source_target_pairs={{0,3},{1,2},{2,1},{3,0},{4,7},{5,6},{6,5},{7,4},{8,11},{9,10},{10,... | collective-permute-start | bytes 1579016 | tf_op jit(solution)/shard_map/cond/branch_0_fun/ppermute | solution.py:957
  372.9 1.9 collective-permute-start
  373.6 6.6 %collective-permute-start.1 = (bf16[512,128]{1,0:T(8,128)(2,1)}, bf16[512,128]{1,0:T(8,128)(2,1)S(1)}, u32[]{:S(2)}, u32[]{:S(2)}) collective-permute-start(bf16[512,128]{1,0:T(8,128)(2,1)} %get-tuple-element.124), channel_id=1, source_target_pairs={{0,8},{4,12},{8,0},{12,4},{16,24},{20,28},{24,16},{28,20},{1,9},{5... | collective-permute-start | bytes 393224 | tf_op jit(solution)/shard_map/cond/branch_0_fun/ppermute | solution.py:957
  374.8 6.3 %collective-permute-start.2 = (bf16[512,128]{1,0:T(8,128)(2,1)}, bf16[512,128]{1,0:T(8,128)(2,1)S(1)}, u32[]{:S(2)}, u32[]{:S(2)}) collective-permute-start(bf16[512,128]{1,0:T(8,128)(2,1)} %get-tuple-element.125), channel_id=1, source_target_pairs={{0,12},{4,8},{8,4},{12,0},{16,28},{20,24},{24,20},{28,16},{1,13},{... | collective-permute-start | bytes 393224 | tf_op jit(solution)/shard_map/cond/branch_0_fun/ppermute | solution.py:957
  380.1 6.3 %collective-permute-start.3 = (bf16[512,128]{1,0:T(8,128)(2,1)}, bf16[512,128]{1,0:T(8,128)(2,1)S(1)}, u32[]{:S(2)}, u32[]{:S(2)}) collective-permute-start(bf16[512,128]{1,0:T(8,128)(2,1)} %get-tuple-element.126), channel_id=1, source_target_pairs={{0,16},{4,20},{8,24},{12,28},{16,0},{20,4},{24,8},{28,12},{1,17},{... | collective-permute-start | bytes 393224 | tf_op jit(solution)/shard_map/cond/branch_0_fun/ppermute | solution.py:957
  381.0 7.4 %collective-permute-start.4 = (bf16[512,128]{1,0:T(8,128)(2,1)}, bf16[512,128]{1,0:T(8,128)(2,1)S(1)}, u32[]{:S(2)}, u32[]{:S(2)}) collective-permute-start(bf16[512,128]{1,0:T(8,128)(2,1)} %get-tuple-element.127), channel_id=1, source_target_pairs={{0,20},{4,16},{8,28},{12,24},{16,4},{20,0},{24,12},{28,8},{1,21},{... | collective-permute-start | bytes 393224 | tf_op jit(solution)/shard_map/cond/branch_0_fun/ppermute | solution.py:957
  386.4 6.1 %collective-permute-start.5 = (bf16[512,128]{1,0:T(8,128)(2,1)}, bf16[512,128]{1,0:T(8,128)(2,1)S(1)}, u32[]{:S(2)}, u32[]{:S(2)}) collective-permute-start(bf16[512,128]{1,0:T(8,128)(2,1)} %get-tuple-element.128), channel_id=1, source_target_pairs={{0,24},{4,28},{8,16},{12,20},{16,8},{20,12},{24,0},{28,4},{1,25},{... | collective-permute-start | bytes 393224 | tf_op jit(solution)/shard_map/cond/branch_0_fun/ppermute | solution.py:957
  388.4 5.5 %collective-permute-start.6 = (bf16[512,128]{1,0:T(8,128)(2,1)}, bf16[512,128]{1,0:T(8,128)(2,1)S(1)}, u32[]{:S(2)}, u32[]{:S(2)}) collective-permute-start(bf16[512,128]{1,0:T(8,128)(2,1)} %get-tuple-element.129), channel_id=1, source_target_pairs={{0,28},{4,24},{8,20},{12,16},{16,12},{20,8},{24,4},{28,0},{1,29},{... | collective-permute-start | bytes 393224 | tf_op jit(solution)/shard_map/cond/branch_0_fun/ppermute | solution.py:957
  (35 other events, 430.2 us)
